TPU v7x, 32 devices: a whole 2x2x4 slice. The times are simulated.
32 devices in a mesh: row: 4 (over y, x), col: 8 (over z, core).
Axes of the slice: x: 2, y: 2, z: 4, core: 2. Of those that a mesh axis runs over, the one named last changes fastest.
Arguments:
- scalar_field: float32 [256, 256, 1024], P('col', 'row'), may hold values from -1.2 to 1.2
- reaction: float32 [256, 256, 1024], P('col', 'row'), may hold values from 0.5 to 4
- x_faces: float32 [1024], replicated, may hold values from 0.5 to 4
- y_faces: float32 [256], replicated, may hold values from 0.5 to 4
- z_faces: float32 [256], replicated, may hold values from 0.5 to 4
- x_inverse: float32 [8, 128, 128], replicated, may hold values from 0 to 1, as said below
- y_inverse: float32 [2, 128, 128], replicated, may hold values from 0 to 1, as said below
- z_inverse: float32 [2, 128, 128], replicated, may hold values from 0 to 1, as said below
Outputs:
- advanced: float32 [256, 256, 1024], P('col', 'row')
Inputs may be any that keep to these rules, and one draw needn't show every extreme that they name: x_inverse[c] is, up to float32 rounding, the inverse of the block of rows and columns c * 128 to (c + 1) * 128 - 1 of the matrix I - 500 A_x along one x line. y_inverse[c] is, up to float32 rounding, the inverse of the block of rows and columns c * 128 to (c + 1) * 128 - 1 of the matrix I - 500 A_y along one y line. z_inverse[c] is, up to float32 rounding, the inverse of the block of rows and columns c * 128 to (c + 1) * 128 - 1 of the matrix I - 500 A_z along one z line.
All inputs are finite; a program needn't handle non-finite values.
Results may differ from a plain program's by a relative error of at most 0.0003.
Values sent between devices are 32-bit elements; how exact they have to be, the bound alone decides.
A program may use at most 128 MiB of HBM per device.

v0:
```python
import jax
import jax.numpy as jnp
from jax import lax
from jax.sharding import PartitionSpec as P

implicit_weight = 0.5
time_step = 1000.0


def with_halo(shard, sides, width):
    for axis, dim in sides:
        size, length = (lax.axis_size(axis), shard.shape[dim])
        up = [(i, (i + 1) % size) for i in range(size - 1)]
        down = [(j, i) for i, j in up]
        last = lax.slice_in_dim(shard, length - width, length, axis=dim)
        leading = lax.slice_in_dim(shard, 0, width, axis=dim)
        before = lax.ppermute(last, axis, up)
        after = lax.ppermute(leading, axis, down)
        shard = jnp.concatenate([before, shard, after], axis=dim)
    return shard


def shift_lower(values, line_axis):
    length = values.shape[line_axis]
    first_slot = jnp.zeros_like(lax.slice_in_dim(values, 0, 1, axis=line_axis))
    return jnp.concatenate(
        [first_slot, lax.slice_in_dim(values, 0, length - 1, axis=line_axis)], axis=line_axis
    )


def shift_upper(values, line_axis):
    length = values.shape[line_axis]
    last_slot = jnp.zeros_like(lax.slice_in_dim(values, 0, 1, axis=line_axis))
    return jnp.concatenate(
        [lax.slice_in_dim(values, 1, length, axis=line_axis), last_slot], axis=line_axis
    )


def apply_line(values, face_values, line_axis):
    spread = [1, 1, 1]
    spread[line_axis] = values.shape[line_axis]
    face_here = face_values.reshape(spread)
    face_next = jnp.concatenate([face_values[1:], jnp.zeros((1,), face_values.dtype)]).reshape(
        spread
    )
    lower_value = shift_lower(values, line_axis)
    upper_value = shift_upper(values, line_axis)
    return face_next * (upper_value - values) - face_here * (values - lower_value)


def invert_small(matrix):
    order = matrix.shape[0]
    joined = jnp.concatenate([matrix, jnp.eye(order, dtype=matrix.dtype)], axis=1)

    def sweep(step_index, current):
        pivot_row = lax.dynamic_index_in_dim(current, step_index, 0, keepdims=False)
        pivot_row = pivot_row / lax.dynamic_index_in_dim(pivot_row, step_index, 0, keepdims=False)
        pivot_column = lax.dynamic_slice_in_dim(current, step_index, 1, 1)
        current = current - pivot_column * pivot_row[None, :]
        return lax.dynamic_update_index_in_dim(current, pivot_row, step_index, 0)

    joined = lax.fori_loop(0, order, sweep, joined)
    return joined[:, order:]


def reduced_inverse(inverse, coupling_before, coupling_after):
    groups, block_width = (inverse.shape[0], inverse.shape[1])
    order = 2 * groups
    group_index = jnp.arange(groups)
    lead_rows = 2 * group_index
    trail_rows = 2 * group_index + 1
    prev_cols = jnp.maximum(2 * group_index - 1, 0)
    next_cols = jnp.minimum(2 * group_index + 2, order - 1)
    coupled = jnp.zeros((order, order), inverse.dtype)
    coupled = coupled.at[lead_rows, prev_cols].add(coupling_before * inverse[:, 0, 0])
    coupled = coupled.at[lead_rows, next_cols].add(coupling_after * inverse[:, 0, block_width - 1])
    coupled = coupled.at[trail_rows, prev_cols].add(
        coupling_before * inverse[:, block_width - 1, 0]
    )
    coupled = coupled.at[trail_rows, next_cols].add(
        coupling_after * inverse[:, block_width - 1, block_width - 1]
    )
    return invert_small(jnp.eye(order, dtype=inverse.dtype) - coupled)


def line_solve(right_side, inverse, face_values, line_axis):
    groups, block_width = (inverse.shape[0], inverse.shape[1])
    dims_full = right_side.shape
    blocked = right_side.reshape(
        dims_full[:line_axis] + (groups, block_width) + dims_full[line_axis + 1 :]
    )
    others = ["u", "v"]
    source = "".join(others[:line_axis] + ["c", "j"] + others[line_axis:])
    target = "".join(others[:line_axis] + ["c", "i"] + others[line_axis:])
    inside = jnp.einsum(
        "cij," + source + "->" + target, inverse, blocked, precision=lax.Precision.HIGHEST
    )
    leading = lax.index_in_dim(inside, 0, line_axis + 1, keepdims=False)
    trailing = lax.index_in_dim(inside, block_width - 1, line_axis + 1, keepdims=False)
    coupling = implicit_weight * time_step * face_values[block_width::block_width]
    nothing = jnp.zeros((1,), face_values.dtype)
    coupling_before = jnp.concatenate([nothing, coupling])
    coupling_after = jnp.concatenate([coupling, nothing])
    reduced = reduced_inverse(inverse, coupling_before, coupling_after)
    interface = jnp.stack([leading, trailing], axis=line_axis + 1)
    interface = interface.reshape(
        dims_full[:line_axis] + (2 * groups,) + dims_full[line_axis + 1 :]
    )
    end_source = "".join(others[:line_axis] + ["j"] + others[line_axis:])
    end_target = "".join(others[:line_axis] + ["i"] + others[line_axis:])
    solved = jnp.einsum(
        "ij," + end_source + "->" + end_target, reduced, interface, precision=lax.Precision.HIGHEST
    )
    solved = solved.reshape(dims_full[:line_axis] + (groups, 2) + dims_full[line_axis + 1 :])
    first_values = lax.index_in_dim(solved, 0, line_axis + 1, keepdims=False)
    last_values = lax.index_in_dim(solved, 1, line_axis + 1, keepdims=False)
    prev_last = shift_lower(last_values, line_axis)
    next_first = shift_upper(first_values, line_axis)
    spike_shape = [1, 1, 1, 1]
    spike_shape[line_axis] = groups
    spike_shape[line_axis + 1] = block_width
    left_spike = (coupling_before[:, None] * inverse[:, :, 0]).reshape(spike_shape)
    right_spike = (coupling_after[:, None] * inverse[:, :, block_width - 1]).reshape(spike_shape)
    result = (
        inside
        + left_spike * jnp.expand_dims(prev_last, line_axis + 1)
        + right_spike * jnp.expand_dims(next_first, line_axis + 1)
    )
    return result.reshape(dims_full)


def body(scalar_field, reaction, x_faces, y_faces, z_faces, x_inverse, y_inverse, z_inverse):
    z_cells, y_cells, x_cells = scalar_field.shape
    padded = with_halo(scalar_field, (("row", 1), ("col", 0)), 1)
    nothing = jnp.zeros((1,), jnp.float32)
    y_padded = jnp.concatenate([y_faces, nothing])
    z_padded = jnp.concatenate([z_faces, nothing])
    y_start = lax.axis_index("row") * y_cells
    z_start = lax.axis_index("col") * z_cells
    y_here = lax.dynamic_slice_in_dim(y_padded, y_start, y_cells).reshape(1, y_cells, 1)
    y_next = lax.dynamic_slice_in_dim(y_padded, y_start + 1, y_cells).reshape(1, y_cells, 1)
    z_here = lax.dynamic_slice_in_dim(z_padded, z_start, z_cells).reshape(z_cells, 1, 1)
    z_next = lax.dynamic_slice_in_dim(z_padded, z_start + 1, z_cells).reshape(z_cells, 1, 1)
    y_term = y_next * (padded[1:-1, 2:, :] - scalar_field) - y_here * (
        scalar_field - padded[1:-1, :-2, :]
    )
    z_term = z_next * (padded[2:, 1:-1, :] - scalar_field) - z_here * (
        scalar_field - padded[:-2, 1:-1, :]
    )
    x_term = apply_line(scalar_field, x_faces, 2)
    source = reaction * scalar_field * (1.0 - scalar_field * scalar_field)
    change = time_step * (x_term + y_term + z_term + source)
    first_section = line_solve(change, x_inverse, x_faces, 2)
    section_y = lax.all_to_all(first_section, "row", split_axis=2, concat_axis=1, tiled=True)
    second_section = line_solve(section_y, y_inverse, y_faces, 1)
    section_z = lax.all_to_all(second_section, "col", split_axis=1, concat_axis=0, tiled=True)
    total_change = line_solve(section_z, z_inverse, z_faces, 0)
    returned = lax.all_to_all(
        lax.all_to_all(total_change, "col", split_axis=0, concat_axis=1, tiled=True),
        "row",
        split_axis=1,
        concat_axis=2,
        tiled=True,
    )
    return scalar_field + returned


def solution(mesh):
    in_specs = (P("col", "row", None), P("col", "row", None), P(), P(), P(), P(), P(), P())
    out_specs = P("col", "row", None)
    return jax.shard_map(body, mesh=mesh, in_specs=in_specs, out_specs=out_specs, check_vma=False)
```

profile of v0, /device:TPU:0, one launch (start us, length us, event | category | flops | bytes accessed | tf_op | source)
XLA Modules:
  0.0 899.9 jit_solution(2791366461174702454)
XLA Ops:
  0.0 1.8 fusion.73
  1.8 1.3 collective-permute-start
  3.1 5.5 collective-permute-start.1
  8.7 13.3 %fusion.72 = (f32[32,64,1023]{2,1,0:T(8,128)}, f32[32,64,1023]{2,1,0:T(8,128)}) fusion(f32[32,64,1024]{2,1,0:T(8,128)} %param.14), kind=kLoop, calls=%fused_computation.182 | loop fusion | bytes 33521664 | tf_op jit(solution)/shard_map/slice | solution.py:35
  22.7 0.9 scatter_fusion
  23.6 0.9 scatter_fusion.1
  24.4 0.9 scatter_fusion.2
  25.3 0.9 scatter_fusion.3
  26.2 32.5 %while.39 = (s32[]{:T(128)}, f32[16,32]{1,0:T(8,128)S(1)}, s32[]{:T(128)}, s32[]{:T(128)}, s32[]{:T(128)}, /*index=5*/s32[]{:T(128)}) while((s32[]{:T(128)}, f32[16,32]{1,0:T(8,128)S(1)}, s32[]{:T(128)}, s32[]{:T(128)}, s32[]{:T(128)}, /*index=5*/s32[]{:T(128)}) %tuple.111), condition=%wide.region_5.6_spmd, body=%wide.region_4.5_spmd.sunk | while | flops 1092 | bytes 5321 | solution.py:62
  59.3 1.1 pad_maximum_fusion.11
  60.4 1.3 collective-permute-start.2
  61.7 3.2 collective-permute-start.3
  66.0 28.5 %fusion.22 = f32[32,64,8,128]{3,1,0,2:T(8,128)S(1)} fusion(f32[8,128,128]{2,1,0:T(8,128)S(1)} %copy-done.2, f32[32,64,1024]{2,1,0:T(8,128)} %param.14, f32[1,66,1024]{2,1,0:T(8,128)S(1)} %collective-permute-done.3, f32[32,1,1024]{2,1,0:T(1,128)S(1)} %copy.140, f32[32,1,1024]{2,1,0:T(1,128)S(1)} %copy.142, f32[1,66,1024]{2,1,0:T(8,128)S(1)} %collective-permute-done.2, ...), kind=kOutput, calls=%fused_computation.55 | convolution fusion | flops 3286237184 | bytes 43262720 | tf_op jit(solution)/shard_map/cij,uvcj->uvci/dot_general | solution.py:95
  94.4 7.9 fusion.71
  102.9 11.9 %pad_maximum_fusion.8 = f32[32,64,8,2]{3,1,0,2:T(8,128)} fusion(f32[32,64,8,1]{3,1,0,2:T(8,128)} %get-tuple-element.190, f32[32,64,8,1]{3,1,0,2:T(8,128)} %get-tuple-element.189), kind=kLoop, calls=%fused_computation.47 | loop fusion | flops 32768 | bytes 262144 | tf_op jit(solution)/shard_map/stack | solution.py:105
  114.8 5.4 copy.147
  120.9 10.5 %multiply_add_fusion.2 = f32[32,64,8,128]{3,1,0,2:T(8,128)} fusion(f32[32,64,8,128]{3,1,0,2:T(8,128)} %copy-done, f32[32,64,8]{1,0,2:T(8,128)S(1)} %concatenate.122.clone, f32[8,128]{1,0:T(8,128)S(1)} %get-tuple-element.229, f32[32,64,8]{1,0,2:T(8,128)S(1)} %concatenate.121.clone, f32[8,128]{1,0:T(8,128)S(1)} %get-tuple-element.230), kind=kLoop, calls=%fused_computation.54 | loop fusion | flops 8388608 | bytes 16916480 | tf_op jit(solution)/shard_map/add | solution.py:125
  131.4 16.2 %copy.183 = f32[32,64,8,128]{1,0,3,2:T(8,128)} copy(f32[32,64,8,128]{3,1,0,2:T(8,128)} %multiply_add_fusion.2) | data formatting | bytes 16777216 | tf_op jit(solution)/shard_map/reshape | solution.py:129
  147.6 14.7 %reshape.391 = f32[4,1,524288]{2,1,0:T(1,128)} reshape(f32[1024,32,64]{2,1,0:T(8,128)} %bitcast.128) | data formatting | bytes 16777216
  162.3 5.8 all-to-all-start
  170.6 0.6 scatter_fusion.8
  171.5 0.6 scatter_fusion.4
  172.3 0.6 scatter_fusion.9
  173.0 0.6 scatter_fusion.5
  173.6 0.6 scatter_fusion.10
  174.2 0.6 scatter_fusion.6
  174.9 0.6 scatter_fusion.11
  175.5 0.6 scatter_fusion.7
  176.8 8.8 while.40
  176.8 0.6 dynamic_slice.112
  177.4 0.6 dynamic-slice_divide_fusion.7
  178.0 0.6 fusion.88
  178.9 0.6 dynamic_slice.112
  179.5 0.6 dynamic-slice_divide_fusion.7
  180.2 0.6 fusion.88
  181.1 0.6 dynamic_slice.112
  181.7 0.6 dynamic-slice_divide_fusion.7
  182.4 0.6 fusion.88
  183.9 0.6 dynamic-slice_divide_fusion.7
  184.6 0.6 fusion.88
  185.5 75.3 %all-to-all-done = f32[4,1,524288]{2,1,0:T(1,128)} async-done(((f32[4,1,524288]{2,1,0:T(1,128)}), f32[4,1,524288]{2,1,0:T(1,128)}, u32[]{:S(2)}, u32[]{:S(2)}) %all-to-all-start) | async-done | bytes 8388640 | tf_op jit(solution)/shard_map/all_to_all | solution.py:154
  261.3 28.3 %reduce.38 = f32[4,524288]{1,0:T(4,128)} reduce(f32[4,1,524288]{2,1,0:T(1,128)} %all-to-all-done, f32[]{:T(128)} %broadcast.1002), dimensions={1}, to_apply=%all_to_all.48.reduce_sub_computation | reduce | bytes 16777220 | tf_op jit(solution)/shard_map/all_to_all | solution.py:154
  289.7 16.8 %reshape.392 = f32[1024,32,64]{2,1,0:T(8,128)} reshape(f32[4,524288]{1,0:T(4,128)} %reduce.38) | data formatting | bytes 16777216
  306.4 13.0 %copy.184 = f32[32,64,4,256]{3,2,1,0:T(4,128)} copy(f32[32,64,4,256]{1,0,3,2:T(8,128)} %bitcast.129) | data formatting | bytes 16777216 | tf_op jit(solution)/shard_map/all_to_all | solution.py:154
  319.4 5.0 copy.156
  324.4 8.6 fusion.25
  333.1 3.4 copy-done.1
  337.5 5.4 multiply_add_fusion.1
  342.8 1.4 copy.162
  344.2 8.3 copy.163
  352.5 8.6 all-to-all-start.1
  361.1 8.1 while.41
  369.7 175.4 %all-to-all-done.1 = f32[32,256,256]{2,0,1:T(8,128)} async-done(((f32[32,256,256]{2,0,1:T(8,128)}), f32[32,256,256]{2,0,1:T(8,128)}, u32[]{:S(2)}, u32[]{:S(2)}) %all-to-all-start.1) | async-done | bytes 8388640 | tf_op jit(solution)/shard_map/all_to_all | solution.py:156
  545.1 8.2 copy.165
  553.3 13.4 %fusion.28 = f32[2,128,32,256]{3,1,2,0:T(8,128)S(1)} fusion(f32[2,128,32,256]{3,2,1,0:T(8,128)S(1)} %bitcast.133, f32[2,128,128]{2,1,0:T(8,128)S(1)} %copy-done.4), kind=kOutput, calls=%fused_computation.57 | convolution fusion | flops 3221225472 | bytes 16908288 | tf_op jit(solution)/shard_map/cij,cjuv->ciuv/dot_general | solution.py:95
  567.6 2.3 multiply_add_fusion
  569.9 5.1 copy.171
  574.9 186.4 %all_to_all.66 = f32[256,32,256]{2,1,0:T(8,128)S(1)} all-to-all(f32[256,32,256]{2,1,0:T(8,128)S(1)} %bitcast.134), channel_id=1, replica_groups=mesh['row'=4,'col'=8] {'col'}, dimensions={0} | all-to-all | bytes 16777216 | tf_op jit(solution)/shard_map/all_to_all | solution.py:159
  761.4 1.7 copy.172
  763.0 4.9 copy.173
  767.9 96.7 %all_to_all.67 = f32[32,256,256]{2,0,1:T(8,128)} all-to-all(f32[32,256,256]{2,0,1:T(8,128)S(1)} %copy.173), channel_id=1, replica_groups=mesh['row'=4,'col'=8] {'row'}, dimensions={1} | all-to-all | bytes 16777216 | tf_op jit(solution)/shard_map/all_to_all | solution.py:158
  864.6 12.2 %copy.175 = f32[32,64,4,256]{3,2,1,0:T(4,128)} copy(f32[32,64,4,256]{3,0,1,2:T(8,128)} %bitcast.137) | data formatting | bytes 16777216 | tf_op jit(solution)/shard_map/all_to_all | solution.py:158
  876.8 10.7 %all_to_all.61 = f32[32,64,1024]{2,1,0:T(8,128)} reshape(f32[32,64,4,256]{3,2,1,0:T(4,128)} %copy.175) | data formatting | bytes 16777216 | tf_op jit(solution)/shard_map/all_to_all | solution.py:158
  887.5 12.1 %add.391 = f32[32,64,1024]{2,1,0:T(8,128)} add(f32[32,64,1024]{2,1,0:T(8,128)} %param.14, f32[32,64,1024]{2,1,0:T(8,128)} %all_to_all.61) | non-fusion elementwise | flops 2097152 | bytes 25165824 | tf_op jit(solution)/shard_map/add | solution.py:165
  (234 shorter events, 50.3 us)
Async XLA Ops:
  1.8 57.2 %collective-permute-start = (f32[32,1,1024]{2,0,1:T(8,128)S(1)}, f32[32,1,1024]{2,0,1:T(8,128)S(1)}, u32[]{:S(2)}, u32[]{:S(2)}) collective-permute-start(f32[32,1,1024]{2,0,1:T(8,128)S(1)} %copy.188), channel_id=1, source_target_pairs={{8,0},{16,8},{24,16},{9,1},{17,9},{25,17},{10,2},{18,10},{26,18},{... | collective-permute-start | bytes 393224 | tf_op jit(solution)/shard_map/ppermute | solution.py:18
  3.1 56.0 %collective-permute-start.1 = (f32[32,1,1024]{2,0,1:T(8,128)S(1)}, f32[32,1,1024]{2,0,1:T(8,128)S(1)}, u32[]{:S(2)}, u32[]{:S(2)}) collective-permute-start(f32[32,1,1024]{2,0,1:T(8,128)S(1)} %copy.189), channel_id=1, source_target_pairs={{0,8},{8,16},{16,24},{1,9},{9,17},{17,25},{2,10},{10,18},{18,26},{... | collective-permute-start | bytes 393224 | tf_op jit(solution)/shard_map/ppermute | solution.py:17
  8.7 13.4 %copy-start.2 = (f32[8,128,128]{2,1,0:T(8,128)S(1)}, f32[8,128,128]{2,1,0:T(8,128)}, u32[]{:S(2)}) copy-start(f32[8,128,128]{2,1,0:T(8,128)} %param.19) | copy-start | bytes 1572868
  8.7 13.8 %copy-start.5 = (f32[1024]{0:T(1024)S(1)}, f32[1024]{0:T(1024)}, u32[]{:S(2)}) copy-start(f32[1024]{0:T(1024)} %param.16) | copy-start | bytes 12292
  8.7 50.1 %copy-start.6 = (f32[256]{0:T(256)S(1)}, f32[256]{0:T(256)}, u32[]{:S(2)}) copy-start(f32[256]{0:T(256)} %param.18) | copy-start | bytes 3076
  8.7 50.1 %copy-start.7 = (f32[256]{0:T(256)S(1)}, f32[256]{0:T(256)}, u32[]{:S(2)}) copy-start(f32[256]{0:T(256)} %param.17) | copy-start | bytes 3076
  60.4 5.1 collective-permute-start.2
  61.7 4.2 collective-permute-start.3
  94.4 8.4 copy-start
  162.3 8.1 copy-start.4
  162.3 9.0 copy-start.3
  162.3 98.6 %all-to-all-start = ((f32[4,1,524288]{2,1,0:T(1,128)}), f32[4,1,524288]{2,1,0:T(1,128)}, u32[]{:S(2)}, u32[]{:S(2)}) async-start(f32[4,1,524288]{2,1,0:T(1,128)} %reshape.391), calls=%async_computation | async-start | bytes 16777216 | tf_op jit(solution)/shard_map/all_to_all | solution.py:154
  333.1 3.4 copy-start.1
  352.5 192.6 %all-to-all-start.1 = ((f32[32,256,256]{2,0,1:T(8,128)}), f32[32,256,256]{2,0,1:T(8,128)}, u32[]{:S(2)}, u32[]{:S(2)}) async-start(f32[32,256,256]{2,0,1:T(8,128)} %copy.163), calls=%async_computation.1 | async-start | bytes 16777216 | tf_op jit(solution)/shard_map/all_to_all | solution.py:156
where the time goes:
time: 905 us; the launch traced here: 900 us
  blocking collectives  283 us (31%)
  waiting for transfers between devices  251 us (28%)
  local copies, waits for them, and re-layouts  174 us (19%)
  other arithmetic  112 us (12%)
  matrix products  51.9 us (6%)
  starting transfers between devices  25.8 us (3%)
    all_to_all x1, blocking collectives, body(): lax.all_to_all(total_change, 'col', split_axis=0, concat_axis=1, tiled=True)  186 us
    all_to_all x1, waiting for transfers between devices, body(): lax.all_to_all(second_section, 'col', split_axis=1, concat_axis=0, tiled=...  175 us
    all_to_all x1, blocking collectives, body(): lax.all_to_all(lax.all_to_all(total_change, 'col', split_axis=0, concat_a...  96.7 us
    all_to_all x1, waiting for transfers between devices, body(): lax.all_to_all(first_section, 'row', split_axis=2, concat_axis=1, tiled=T...  75.3 us
    dot_general x3, matrix products, line_solve(): jnp.einsum('cij,' + source + '->' + target, inverse, blocked, precision=l...  50.5 us
    unnamed x28, local copies, waits for them, and re-layouts  35.9 us
    all_to_all x1, other arithmetic, body(): lax.all_to_all(first_section, 'row', split_axis=2, concat_axis=1, tiled=T...  28.3 us
    reshape x2, local copies, waits for them, and re-layouts, line_solve(): return result.reshape(dims_full)  24.5 us
  transfers between devices with their start and end apart: 6, of which 3 were waited for; matrix products, arithmetic and copies ran while one was open for 8% of the time, Pallas kernels for 0%

commit v1 on v0

v1 whole, which is shorter than its diff:
```python
import functools

import jax
import jax.numpy as jnp
from jax import lax
from jax.experimental import pallas as pl
from jax.experimental.pallas import tpu as pltpu
from jax.sharding import PartitionSpec as P

WEIGHT = 0.5
STEP = 1000.0
MESH = pl.DeviceIdType.MESH
VMEM_LIMIT = 60 * 1024 * 1024


def shifted(a, by, fill):
    n = a.shape[1]
    lane = lax.broadcasted_iota(jnp.int32, a.shape, 1)
    if by > 0:
        return jnp.where(lane >= by, pltpu.roll(a, by, 1), fill)
    return jnp.where(lane < n + by, pltpu.roll(a, n + by, 1), fill)


def running_sum(a):
    by = 1
    while by < a.shape[1]:
        a = a + shifted(a, by, 0.0)
        by *= 2
    return a


def ladder(couple, sign):
    p00, p01, p10, p11 = 1.0 + couple, couple, jnp.ones_like(couple), couple
    by = 1
    while by < couple.shape[1]:
        q00, q01 = shifted(p00, sign * by, 1.0), shifted(p01, sign * by, 0.0)
        q10, q11 = shifted(p10, sign * by, 0.0), shifted(p11, sign * by, 1.0)
        n00, n01 = p00 * q00 + p01 * q10, p00 * q01 + p01 * q11
        n10, n11 = p10 * q00 + p11 * q10, p10 * q01 + p11 * q11
        scale = 1.0 / (n00 + n01 + n10 + n11)
        p00, p01, p10, p11 = n00 * scale, n01 * scale, n10 * scale, n11 * scale
        by *= 2
    return p00 / p10


def ladder_kernel(faces_ref, out_ref):
    here = WEIGHT * STEP * faces_ref[...]
    above = shifted(here, -1, 0.0)
    e = ladder(here, 1)
    h = ladder(above, -1)
    pivot = above + e
    up = here / (here + h)
    down = above / pivot
    out_ref[0:8] = 1.0 / (e + h - 1.0)
    out_ref[8:16] = running_sum(jnp.log(jnp.maximum(up, 1e-30)))
    out_ref[16:24] = running_sum(jnp.log(jnp.maximum(down, 1e-30)))
    out_ref[24:32] = 1.0 / pivot
    out_ref[32:40] = down


def split(a):
    high = a.astype(jnp.bfloat16)
    return high, (a - high.astype(jnp.float32)).astype(jnp.bfloat16)


def dot(a, b):
    return jnp.dot(a, b, preferred_element_type=jnp.float32)


def sweep_kernel(
    planes, zco_ref, kz_ref, u_ref, before_ref, after_ref, zlo_ref, zhi_ref, ylo_ref, yhi_ref,
    rea_ref, kx_ref, ky_ref, xh_ref, xl_ref, xp_ref, ym_ref, v_ref, ye_ref, ze_ref,
):
    step, steps = pl.program_id(0), pl.num_programs(0)
    _, yc, nx = u_ref.shape
    zc = v_ref.shape[0]
    nb, bx = xh_ref.shape[0], xh_ref.shape[1]
    kx, kxn = kx_ref[0:1], kx_ref[1:2]
    ky, kyn = ky_ref[:, 0:1], ky_ref[:, 1:2]
    lane = lax.broadcasted_iota(jnp.int32, (yc, nx), 1)
    sub = lax.broadcasted_iota(jnp.int32, (yc, nx), 0)

    @pl.when(step == 0)
    def _():
        v_ref[0] = jnp.zeros((yc, nx), jnp.float32)

    below = jnp.where(step == 0, zlo_ref[0], before_ref[0])
    above_last = jnp.where(step == steps - 1, zhi_ref[0], after_ref[0])
    changes = []
    for p in range(planes):
        z = step * planes + p
        u = u_ref[p]
        above = u_ref[p + 1] if p + 1 < planes else above_last
        left = jnp.where(lane == 0, 0.0, pltpu.roll(u, 1, 1))
        right = pltpu.roll(u, nx - 1, 1)
        down = jnp.where(sub == 0, ylo_ref[p], pltpu.roll(u, 1, 0))
        upper = jnp.where(sub == yc - 1, yhi_ref[p], pltpu.roll(u, yc - 1, 0))
        total = kxn * (right - u) - kx * (u - left)
        total += kyn * (upper - u) - ky * (u - down)
        total += kz_ref[1, z] * (above - u) - kz_ref[0, z] * (u - below)
        total += rea_ref[p] * u * (1.0 - u * u)
        changes.append(STEP * total)
        below = u
    change = jnp.concatenate(changes, axis=0) if planes > 1 else changes[0]
    local = []
    for b in range(nb):
        high, low = split(change[:, b * bx:(b + 1) * bx])
        local.append(dot(high, xh_ref[b]) + (dot(high, xl_ref[b]) + dot(low, xh_ref[b])))
    rows = planes * yc
    from_left = [jnp.zeros((rows, 1), jnp.float32)]
    from_right = [jnp.zeros((rows, 1), jnp.float32)]
    for b in range(nb - 1):
        through = xp_ref[0:1, (b + 1) * bx - 1:(b + 1) * bx]
        from_left.append(from_left[-1] * through + local[b][:, bx - 1:bx])
        c = nb - 1 - b
        through = xp_ref[1:2, c * bx:c * bx + 1]
        from_right.append(from_right[-1] * through + local[c][:, 0:1])
    from_right.reverse()
    solved = jnp.concatenate(
        [
            local[b]
            + xp_ref[0:1, b * bx:(b + 1) * bx] * from_left[b]
            + xp_ref[1:2, b * bx:(b + 1) * bx] * from_right[b]
            for b in range(nb)
        ],
        axis=1,
    )
    carry = v_ref[jnp.maximum(step * planes - 1, 0)]
    for p in range(planes):
        z = step * planes + p
        high, low = split(solved[p * yc:(p + 1) * yc])
        w = dot(ym_ref[...], jnp.concatenate([high, low, high], axis=0))
        carry = zco_ref[0, z] * w + zco_ref[1, z] * carry
        v_ref[z] = carry

    @pl.when(step == steps - 1)
    def _():
        wide = 256 if nx % 256 == 0 else nx
        for x in range(nx // wide):
            cols = slice(x * wide, (x + 1) * wide)
            top = v_ref[zc - 1, :, cols]
            ze_ref[1, :, cols] = top
            ye_ref[0, zc - 1:zc, cols] = top[0:1]
            ye_ref[1, zc - 1:zc, cols] = top[yc - 1:yc]

            def back(i, value):
                z = zc - 2 - i
                value = v_ref[z, :, cols] + zco_ref[2, z] * value
                v_ref[z, :, cols] = value
                ye_ref[0, pl.ds(z, 1), cols] = value[0:1]
                ye_ref[1, pl.ds(z, 1), cols] = value[yc - 1:yc]
                return value

            ze_ref[0, :, cols] = lax.fori_loop(0, zc - 1, back, top)


def exchange_kernel(
    nr, nc, chunks, yw_ref, zw_ref, yp_ref, ye_ref, ze_ref, sy_ref, sz_ref,
    ybuf, zbuf, zsend, ysend_sem, yrecv_sem, zsend_sem, zrecv_sem,
):
    row, col = lax.axis_index("row"), lax.axis_index("col")
    zc, nx = ye_ref.shape[1], ye_ref.shape[2]
    yc = ze_ref.shape[1]
    has_low, has_high = col > 0, col < nc - 1
    barrier = pltpu.get_barrier_semaphore()
    for other in range(nr):
        @pl.when(other != row)
        def _():
            pl.semaphore_signal(barrier, inc=1, device_id=(other, col), device_id_type=MESH)

    @pl.when(has_low)
    def _():
        pl.semaphore_signal(barrier, inc=1, device_id=(row, col - 1), device_id_type=MESH)

    @pl.when(has_high)
    def _():
        pl.semaphore_signal(barrier, inc=1, device_id=(row, col + 1), device_id_type=MESH)

    pl.semaphore_wait(barrier, nr - 1 + has_low.astype(jnp.int32) + has_high.astype(jnp.int32))

    def y_copy(side, other, slot):
        return pltpu.make_async_remote_copy(
            src_ref=ye_ref.at[1 - side],
            dst_ref=ybuf.at[side, slot],
            send_sem=ysend_sem.at[side, other],
            recv_sem=yrecv_sem.at[side, slot],
            device_id=(other, col),
            device_id_type=MESH,
        )

    for other in range(nr):
        @pl.when(other > row)
        def _():
            y_copy(0, other, row).start()

        @pl.when(other < row)
        def _():
            y_copy(1, other, row).start()

    sy_ref[...] = jnp.zeros_like(sy_ref)
    for other in range(nr):
        @pl.when(other < row)
        def _():
            y_copy(0, other, other).wait_recv()
            sy_ref[0] += yw_ref[0, other] * ybuf[0, other]

        @pl.when(other > row)
        def _():
            y_copy(1, other, other).wait_recv()
            sy_ref[1] += yw_ref[1, other] * ybuf[1, other]

    yb, ya = yp_ref[:, 0:1], yp_ref[:, 1:2]
    part = yc // chunks

    def z_copy(side, k):
        rows = pl.ds(k * part, part)
        return pltpu.make_async_remote_copy(
            src_ref=zsend.at[side, rows],
            dst_ref=zbuf.at[side, rows],
            send_sem=zsend_sem.at[side, k],
            recv_sem=zrecv_sem.at[side, k],
            device_id=(row, col + (1 - 2 * side)),
            device_id_type=MESH,
        )

    def scan(side):
        source, target = (has_low, has_high) if side == 0 else (has_high, has_low)
        edge, z = (1, zc - 1) if side == 0 else (0, 0)
        for k in range(chunks):
            rows = slice(k * part, (k + 1) * part)

            @pl.when(source)
            def _():
                z_copy(side, k).wait_recv()
                sz_ref[side, rows] = zbuf[side, rows]

            @pl.when(jnp.logical_not(source))
            def _():
                sz_ref[side, rows] = jnp.zeros((part, nx), jnp.float32)

            @pl.when(target)
            def _():
                value = ze_ref[edge, rows] + yb[rows] * sy_ref[0, z:z + 1]
                value += ya[rows] * sy_ref[1, z:z + 1]
                zsend[side, rows] = value + zw_ref[side] * sz_ref[side, rows]
                z_copy(side, k).start()

    low_half = col < nc // 2

    @pl.when(low_half)
    def _():
        scan(0)

    scan(1)

    @pl.when(jnp.logical_not(low_half))
    def _():
        scan(0)

    for k in range(chunks):
        @pl.when(has_high)
        def _():
            z_copy(0, k).wait_send()

        @pl.when(has_low)
        def _():
            z_copy(1, k).wait_send()

    for other in range(nr):
        @pl.when(other > row)
        def _():
            y_copy(0, other, row).wait_send()

        @pl.when(other < row)
        def _():
            y_copy(1, other, row).wait_send()


def finish_kernel(planes, zp_ref, u_ref, v_ref, yp_ref, sy_ref, sz_ref, out_ref):
    yb, ya = yp_ref[:, 0:1], yp_ref[:, 1:2]
    for p in range(planes):
        z = pl.program_id(0) * planes + p
        value = u_ref[p] + v_ref[p]
        value += yb * sy_ref[0, pl.ds(z, 1)] + ya * sy_ref[1, pl.ds(z, 1)]
        out_ref[p] = value + zp_ref[0, z] * sz_ref[0] + zp_ref[1, z] * sz_ref[1]


def blocks_of_inverse(diagonal, sums):
    n = diagonal.shape[-1]
    i = lax.broadcasted_iota(jnp.int32, (n, n), 0)
    j = lax.broadcasted_iota(jnp.int32, (n, n), 1)
    near = jnp.where(i >= j, diagonal[..., None, :], diagonal[..., :, None])
    return near * jnp.exp(-jnp.abs(sums[..., :, None] - sums[..., None, :]))


def halves(a):
    high = lax.reduce_precision(a, 8, 7)
    return high.astype(jnp.bfloat16), (a - high).astype(jnp.bfloat16)


def body(u, reaction, x_faces, y_faces, z_faces, x_inverse, y_inverse, z_inverse):
    zc, yc, nx = u.shape
    nr, nc = lax.axis_size("row"), lax.axis_size("col")
    row, col = lax.axis_index("row"), lax.axis_index("col")
    ny, nz = y_faces.shape[0], z_faces.shape[0]
    f32 = jnp.float32

    def up(n):
        return [(i, i + 1) for i in range(n - 1)]

    def down(n):
        return [(i + 1, i) for i in range(n - 1)]

    ylo = lax.ppermute(u[:, yc - 1:yc], "row", up(nr))
    yhi = lax.ppermute(u[:, 0:1], "row", down(nr))
    zlo = lax.ppermute(u[zc - 1:zc], "col", up(nc))
    zhi = lax.ppermute(u[0:1], "col", down(nc))

    longest = -(-max(nx, ny, nz) // 128) * 128
    faces = jnp.stack([jnp.pad(f, (0, longest - f.shape[0])) for f in (x_faces, y_faces, z_faces)])
    faces = jnp.pad(faces, ((0, 5), (0, 0)))
    tables = pl.pallas_call(
        ladder_kernel, out_shape=jax.ShapeDtypeStruct((40, longest), f32)
    )(faces).reshape(5, 8, longest)

    bx = 256 if nx % 256 == 0 else nx
    nb = nx // bx
    diag, up_sum, down_sum = (tables[i, 0, :nx].reshape(nb, bx) for i in range(3))
    xh, xl = halves(blocks_of_inverse(diag, up_sum))
    zero = jnp.zeros((1,), f32)
    up_start = jnp.concatenate([zero, up_sum[:-1, -1]])[:, None]
    down_before = jnp.concatenate([zero, tables[2, 0, :nx - 1]]).reshape(nb, bx)
    xp = jnp.stack([jnp.exp(up_sum - up_start), jnp.exp(down_sum[:, -1:] - down_before)])
    xp = xp.reshape(2, nx)
    kx = jnp.stack([x_faces, jnp.concatenate([x_faces[1:], zero])])

    def own(values, start, count):
        return lax.dynamic_slice_in_dim(values, start, count)

    def passes(which, n, start, count):
        ups = jnp.concatenate([zero, tables[1, which, :n]])
        downs = jnp.concatenate([zero, tables[2, which, :n]])
        ups_here, downs_here = own(ups, start, count + 1), own(downs, start, count + 1)
        onward = jnp.exp(ups_here[1:] - ups_here[0])
        backward = jnp.exp(downs_here[count] - downs_here[:count])
        return ups, downs, ups_here, downs_here, onward, backward

    y0 = row * yc
    ups, downs, ups_here, downs_here, onward, backward = passes(1, ny, y0, yc)
    yh, yl = halves(blocks_of_inverse(own(tables[0, 1, :ny], y0, yc), ups_here[1:]))
    ym = jnp.concatenate([yh, yh, yl], axis=1)
    yp = jnp.stack([onward, backward], axis=1)
    who = jnp.arange(nr)
    from_low = jnp.where(who < row, jnp.exp(jnp.minimum(ups_here[0] - ups[yc::yc], 0.0)), 0.0)
    from_high = jnp.where(who > row, jnp.exp(jnp.minimum(downs[:-1:yc] - downs_here[yc], 0.0)), 0.0)
    yw = jnp.stack([from_low, from_high])
    yf = jnp.concatenate([y_faces, zero])
    ky = jnp.stack([own(yf, y0, yc), own(yf, y0 + 1, yc)], axis=1)

    z0 = col * zc
    _, _, _, _, z_onward, z_backward = passes(2, nz, z0, zc)
    zp = jnp.stack([z_onward, z_backward])
    zw = jnp.stack([z_onward[-1], z_backward[0]])
    zf = jnp.concatenate([z_faces, zero])
    kz = jnp.stack([own(zf, z0, zc), own(zf, z0 + 1, zc)])
    at = jnp.arange(zc)
    over = jnp.where(at == zc - 1, own(tables[0, 2, :nz], z0, zc), own(tables[3, 2, :nz], z0, zc))
    into = jnp.where(at == 0, 0.0, WEIGHT * STEP * kz[0] * over)
    zco = jnp.stack([over, into, own(tables[4, 2, :nz], z0, zc)])

    planes = 2 if zc % 2 == 0 else 1
    steps = zc // planes
    smem = pl.BlockSpec(memory_space=pltpu.SMEM)
    vmem = pl.BlockSpec(memory_space=pltpu.VMEM)
    plane = (1, yc, nx)

    def whole(*shape):
        return pl.BlockSpec(shape, lambda s: (0,) * len(shape))

    slab = pl.BlockSpec((planes, yc, nx), lambda s: (s, 0, 0))
    line = pl.BlockSpec((planes, 1, nx), lambda s: (s, 0, 0))
    v, ye, ze = pl.pallas_call(
        functools.partial(sweep_kernel, planes),
        grid=(steps,),
        in_specs=[
            smem, smem, slab,
            pl.BlockSpec(plane, lambda s: (jnp.maximum(s * planes - 1, 0), 0, 0)),
            pl.BlockSpec(plane, lambda s: (jnp.minimum((s + 1) * planes, zc - 1), 0, 0)),
            whole(*plane), whole(*plane), line, line, slab,
            whole(2, nx), whole(yc, 2), whole(nb, bx, bx), whole(nb, bx, bx), whole(2, nx),
            whole(yc, 3 * yc),
        ],
        out_specs=[whole(zc, yc, nx), whole(2, zc, nx), whole(2, yc, nx)],
        out_shape=[
            jax.ShapeDtypeStruct((zc, yc, nx), f32),
            jax.ShapeDtypeStruct((2, zc, nx), f32),
            jax.ShapeDtypeStruct((2, yc, nx), f32),
        ],
        compiler_params=pltpu.CompilerParams(vmem_limit_bytes=VMEM_LIMIT),
    )(zco, kz, u, u, u, zlo, zhi, ylo, yhi, reaction, kx, ky, xh, xl, xp, ym)

    chunks = 4 if yc % 32 == 0 else 1
    sy, sz = pl.pallas_call(
        functools.partial(exchange_kernel, nr, nc, chunks),
        in_specs=[smem, smem, vmem, vmem, vmem],
        out_specs=[vmem, vmem],
        out_shape=[
            jax.ShapeDtypeStruct((2, zc, nx), f32),
            jax.ShapeDtypeStruct((2, yc, nx), f32),
        ],
        scratch_shapes=[
            pltpu.VMEM((2, nr, zc, nx), f32),
            pltpu.VMEM((2, yc, nx), f32),
            pltpu.VMEM((2, yc, nx), f32),
            pltpu.SemaphoreType.DMA((2, nr)),
            pltpu.SemaphoreType.DMA((2, nr)),
            pltpu.SemaphoreType.DMA((2, chunks)),
            pltpu.SemaphoreType.DMA((2, chunks)),
        ],
        compiler_params=pltpu.CompilerParams(
            collective_id=0, has_side_effects=True, vmem_limit_bytes=VMEM_LIMIT
        ),
    )(yw, zw, yp, ye, ze)

    return pl.pallas_call(
        functools.partial(finish_kernel, planes),
        grid=(steps,),
        in_specs=[smem, slab, slab, whole(yc, 2), whole(2, zc, nx), whole(2, yc, nx)],
        out_specs=slab,
        out_shape=jax.ShapeDtypeStruct((zc, yc, nx), f32),
        compiler_params=pltpu.CompilerParams(vmem_limit_bytes=VMEM_LIMIT),
    )(zp, u, v, yp, sy, sz)


def solution(mesh):
    in_specs = (P("col", "row", None), P("col", "row", None), P(), P(), P(), P(), P(), P())
    out_specs = P("col", "row", None)
    return jax.shard_map(body, mesh=mesh, in_specs=in_specs, out_specs=out_specs, check_vma=False)
```

time: 905 us -> 116 us (0.13)
  blocking collectives: 283 us -> 0 us
  waiting for transfers between devices: 251 us -> 0.01 us
  local copies, waits for them, and re-layouts: 174 us -> 12.7 us
  other arithmetic: 112 us -> 14 us
  Pallas kernels: 0 us -> 76.5 us
  matrix products: 51.9 us -> 0 us
  starting transfers between devices: 25.8 us -> 11.1 us
    all_to_all x2 -> x0, blocking collectives: 283 us -> none  [the longest x1 186 us: body(): lax.all_to_all(total_change, 'col', split_axis=0, concat_axis=1, tiled=True)]
    all_to_all x2 -> x0, waiting for transfers between devices: 251 us -> none  [the longest x1 175 us: body(): lax.all_to_all(second_section, 'col', split_axis=1, concat_axis=0, tiled=...]
    pallas_call x0 -> x4, Pallas kernels: none -> 76.5 us  [the longest x1 29.4 us: body(): pl.pallas_call(functools.partial(sweep_kernel, planes), grid=(steps,), in...]
    all_to_all x8 -> x0, local copies, waits for them, and re-layouts: 56.1 us -> none  [the longest x2 22.9 us: body(): lax.all_to_all(lax.all_to_all(total_change, 'col', split_axis=0, concat_a...]
    dot_general x6 -> x0, matrix products: 51.9 us -> none  [the longest x3 50.5 us: line_solve(): jnp.einsum('cij,' + source + '->' + target, inverse, blocked, precision=l...]
    unnamed x28 -> x14, local copies, waits for them, and re-layouts: 35.9 us -> 1.19 us
    add x4 -> x0, other arithmetic: 30.3 us -> none  [the longest x3 18.2 us: line_solve(): inside + left_spike * jnp.expand_dims(prev_last, line_axis + 1)]
    all_to_all x1 -> x0, other arithmetic: 28.3 us -> none  [body(): lax.all_to_all(first_section, 'row', split_axis=2, concat_axis=1, tiled=T...]
  transfers between devices with their start and end apart: 6 -> 4, of which waited for: 3 -> 0; matrix products, arithmetic and copies ran while one was open for 8% -> 21% of each run, Pallas kernels for 0% -> 2%
where the time goes in v1:
time: 116 us; the launch traced here: 114 us
  Pallas kernels  76.5 us (66%)
  other arithmetic  14 us (12%)
  local copies, waits for them, and re-layouts  12.7 us (11%)
  starting transfers between devices  11.1 us (10%)
    pallas_call x1, Pallas kernels, body(): pl.pallas_call(functools.partial(sweep_kernel, planes), grid=(steps,), in...  29.4 us
    pallas_call x1, Pallas kernels, body(): pl.pallas_call(functools.partial(exchange_kernel, nr, nc, chunks), in_spe...  28.9 us
    pallas_call x1, Pallas kernels, body(): pl.pallas_call(functools.partial(finish_kernel, planes), grid=(steps,), i...  15.3 us
    ppermute x1, starting transfers between devices, body(): ylo = lax.ppermute(u[:, yc - 1:yc], 'row', up(nr))  5.51 us
    ppermute x1, starting transfers between devices, body(): zlo = lax.ppermute(u[zc - 1:zc], 'col', up(nc))  3.05 us
    pallas_call x1, Pallas kernels, body(): pl.pallas_call(ladder_kernel, out_shape=jax.ShapeDtypeStruct((40, longest...  2.82 us
  transfers between devices with their start and end apart: 4, of which 0 were waited for; matrix products, arithmetic and copies ran while one was open for 21% of the time, Pallas kernels for 2%

profile of v1, /device:TPU:0, one launch (start us, length us, event | category | flops | bytes accessed | tf_op | source)
XLA Modules:
  0.0 114.4 jit_solution(13594359752486138266)
XLA Ops:
  0.0 1.8 %fusion.10 = (f32[32,1,1024]{2,1,0:T(1,128)S(1)}, f32[32,1,1024]{2,1,0:T(1,128)S(1)}) fusion(f32[32,64,1024]{2,1,0:T(8,128)} %u_ref.3), kind=kLoop, calls=%fused_computation.64 | loop fusion | bytes 524288 | tf_op jit(solution)/shard_map/slice | solution.py:315
  1.8 1.3 %collective-permute-start.3 = (f32[32,1,1024]{2,1,0:T(1,128)S(1)}, f32[32,1,1024]{2,1,0:T(1,128)S(1)}, u32[]{:S(2)}, u32[]{:S(2)}) collective-permute-start(f32[32,1,1024]{2,1,0:T(1,128)S(1)} %get-tuple-element.18), channel_id=1, source_target_pairs={{8,0},{16,8},{24,16},{9,1},{17,9},{25,17},{10,2},{18,10},{26,18},{... | collective-permute-start | bytes 393224 | tf_op jit(solution)/shard_map/ppermute | solution.py:315
  3.1 5.5 %collective-permute-start.2 = (f32[32,1,1024]{2,1,0:T(1,128)S(1)}, f32[32,1,1024]{2,1,0:T(1,128)S(1)}, u32[]{:S(2)}, u32[]{:S(2)}) collective-permute-start(f32[32,1,1024]{2,1,0:T(1,128)S(1)} %get-tuple-element.19), channel_id=1, source_target_pairs={{0,8},{8,16},{16,24},{1,9},{9,17},{17,25},{2,10},{10,18},{18,26},{... | collective-permute-start | bytes 393224 | tf_op jit(solution)/shard_map/ppermute | solution.py:314
  8.6 1.1 fusion.11
  9.7 1.3 %collective-permute-start.1 = (f32[1,64,1024]{2,1,0:T(8,128)S(1)}, f32[1,64,1024]{2,1,0:T(8,128)S(1)}, u32[]{:S(2)}, u32[]{:S(2)}) collective-permute-start(f32[1,64,1024]{2,1,0:T(8,128)S(1)} %get-tuple-element.20), channel_id=1, source_target_pairs={{1,0},{2,1},{3,2},{4,3},{5,4},{6,5},{7,6},{9,8},{10,9},{11,10},{12... | collective-permute-start | bytes 786440 | tf_op jit(solution)/shard_map/ppermute | solution.py:317
  11.0 3.0 %collective-permute-start = (f32[1,64,1024]{2,1,0:T(8,128)S(1)}, f32[1,64,1024]{2,1,0:T(8,128)S(1)}, u32[]{:S(2)}, u32[]{:S(2)}) collective-permute-start(f32[1,64,1024]{2,1,0:T(8,128)S(1)} %get-tuple-element.21), channel_id=1, source_target_pairs={{0,1},{1,2},{2,3},{3,4},{4,5},{5,6},{6,7},{8,9},{9,10},{10,11},{11... | collective-permute-start | bytes 786440 | tf_op jit(solution)/shard_map/ppermute | solution.py:316
  14.1 0.8 slice.111
  14.8 0.7 pad.11
  15.5 0.7 pad.12
  16.2 1.3 %select_maximum_fusion.faces_ref = f32[8,1024]{1,0:T(8,128)} fusion(f32[1,1024]{1,0:T(1,128)S(1)} %bitcast.76, f32[1,1024]{1,0:T(1,128)S(1)} %bitcast.75, f32[1,1024]{1,0:T(1,128)} %bitcast.70), kind=kLoop, calls=%fused_computation.8 | loop fusion | flops 49152 | bytes 45056 | tf_op jit(solution)/shard_map/stack | solution.py:320
  17.5 2.8 %shard_map.55 = f32[40,1024]{1,0:T(8,128)} custom-call(f32[8,1024]{1,0:T(8,128)} %select_maximum_fusion.faces_ref), custom_call_target="tpu_custom_call" | custom-call | tf_op jit(solution)/shard_map/pallas_call | solution.py:322
  20.3 0.8 slice_bitcast_fusion
  21.1 0.8 fusion.12
  21.9 0.7 pad_maximum_fusion.8
  22.6 0.1 pad_maximum_fusion.5
  22.7 0.1 dynamic_slice.44
  22.8 0.1 fusion.13
  22.9 0.1 subtract_exponential_fusion.1
  23.0 0.1 dynamic_slice.45
  23.1 0.6 slice.102
  23.7 0.6 fusion.14
  24.3 0.6 subtract_exponential_fusion
  25.0 0.8 slice_reduce_fusion
  25.8 0.1 pad_maximum_fusion.7
  25.9 1.3 %pad_maximum_fusion.1.kx_ref = f32[2,1024]{1,0:T(2,128)} fusion(f32[1,1024]{1,0:T(1,128)S(1)} %bitcast.74, f32[1,1024]{1,0:T(1,128)} %bitcast.71), kind=kLoop, calls=%fused_computation.14 | loop fusion | flops 2048 | bytes 16384 | tf_op jit(solution)/shard_map/stack | solution.py:335
  27.2 0.1 slice.126
  27.2 0.1 pad_maximum_fusion.3
  27.3 0.1 slice.127
  27.4 0.1 dynamic_slice.59
  27.5 0.1 dynamic_slice.58
  27.6 0.6 slice.124
  28.2 0.6 exponential_bitcast_fusion
  28.8 0.6 fusion.9
  29.5 0.1 exponential_bitcast_fusion.1
  29.6 0.1 slice.139
  29.7 0.1 copy.18
  29.8 0.1 broadcast_bitcast_fusion
  29.9 0.1 slice.137
  30.0 0.1 copy.17
  30.1 0.1 pad_maximum_fusion.16
  30.1 0.1 broadcast_bitcast_fusion.1
  30.2 0.1 dynamic-slice_bitcast_fusion.1
  30.3 0.1 fusion.4
  30.4 0.1 compare_select_fusion.4
  30.5 0.1 dynamic-slice_bitcast_fusion.3
  30.6 0.6 pad_maximum_fusion.12.kz_ref
  31.2 0.6 pad_maximum_fusion.15.yw_ref
  31.8 0.8 fusion.2
  32.7 0.6 pad_maximum_fusion.2.xp_ref
  33.3 0.1 reduce-precision_convert_fusion.1
  33.4 1.4 %fusion = (bf16[4,256,256]{2,1,0:T(8,128)(2,1)}, bf16[4,256,256]{2,1,0:T(8,128)(2,1)}) fusion(f32[4,256]{1,0:T(4,128)S(1)} %sub.110, f32[4,256]{1,0:T(4,128)S(1)} %broadcast_in_dim.54, pred[256,256]{1,0:T(8,128)(4,1)S(1)} %iota_compare_fusion), kind=kLoop, calls=%fused_computation.2 | loop fusion | flops 2359296 | bytes 1122304 | tf_op jit(solution)/shard_map/convert_element_type | solution.py:298
  34.7 0.6 pad_maximum_fusion.10.zco_ref
  35.3 0.5 pad_maximum_fusion.11.zp_ref
  35.9 0.6 slice.128
  36.5 1.3 %pad_maximum_fusion.17.zw_ref = f32[2]{0:T(128)} fusion(f32[1]{0:T(128)S(1)} %bitcast.86, f32[1]{0:T(128)} %slice.128), kind=kLoop, calls=%fused_computation.55 | loop fusion | flops 2 | bytes 16 | tf_op jit(solution)/shard_map/stack | solution.py:363
  37.8 0.7 copy.14.ky_ref
  38.5 0.7 copy.16.yp_ref
  39.2 0.7 pad_maximum_fusion.ym_ref
  39.9 0.6 copy-done.2
  40.6 0.1 copy-done
  40.7 0.1 copy-done.1
  40.8 29.4 %shard_map.56 = (f32[32,64,1024]{2,1,0:T(8,128)}, f32[2,32,1024]{2,1,0:T(8,128)}, f32[2,64,1024]{2,1,0:T(8,128)}) custom-call(f32[3,32]{1,0:T(4,128)} %pad_maximum_fusion.10.zco_ref, f32[2,32]{1,0:T(2,128)} %pad_maximum_fusion.12.kz_ref, f32[32,64,1024]{2,1,0:T(8,128)} %u_ref.3, f32[32,64,1024]{2,1,0:T(8,128)} %u_ref.3, f32[32,64,1024]{2,1,0:T(8,128)} %u_ref.3, ...), custom_call_target="tpu_custom_call" | custom-call | tf_op jit(solution)/shard_map/pallas_call | solution.py:382
  70.2 28.9 %shard_map.57 = (f32[2,32,1024]{2,1,0:T(8,128)}, f32[2,64,1024]{2,1,0:T(8,128)}) custom-call(f32[2,4]{1,0:T(2,128)} %pad_maximum_fusion.15.yw_ref, f32[2]{0:T(128)} %pad_maximum_fusion.17.zw_ref, f32[64,2]{1,0:T(8,128)} %copy.16.yp_ref, f32[2,32,1024]{2,1,0:T(8,128)} %get-tuple-element.11.ye_ref, f32[2,64,1024]{2,1,0:T(8,128)} %get-tuple-element.12.ze_ref), custom_call_target="tpu_custom_call" | custom-call | tf_op jit(solution)/shard_map/pallas_call | solution.py:403
  99.1 15.3 %shard_map.58 = f32[32,64,1024]{2,1,0:T(8,128)} custom-call(f32[2,32]{1,0:T(2,128)} %pad_maximum_fusion.11.zp_ref, f32[32,64,1024]{2,1,0:T(8,128)} %u_ref.3, f32[32,64,1024]{2,1,0:T(8,128)} %get-tuple-element.10.v_ref, f32[64,2]{1,0:T(8,128)} %copy.16.yp_ref, f32[2,32,1024]{2,1,0:T(8,128)} %get-tuple-element.13.sy_ref, f32[2,64,1024]{2,1,0:T(8,128)} %get-tuple-element.14.sz_ref), custom_call_target="tpu_custom_call" | custom-call | tf_op jit(solution)/shard_map/pallas_call | solution.py:425
  (19 shorter events, 0.3 us)
Async XLA Ops:
  1.8 38.1 %collective-permute-start.3 = (f32[32,1,1024]{2,1,0:T(1,128)S(1)}, f32[32,1,1024]{2,1,0:T(1,128)S(1)}, u32[]{:S(2)}, u32[]{:S(2)}) collective-permute-start(f32[32,1,1024]{2,1,0:T(1,128)S(1)} %get-tuple-element.18), channel_id=1, source_target_pairs={{8,0},{16,8},{24,16},{9,1},{17,9},{25,17},{10,2},{18,10},{26,18},{... | collective-permute-start | bytes 393224 | tf_op jit(solution)/shard_map/ppermute | solution.py:315
  3.1 36.8 %collective-permute-start.2 = (f32[32,1,1024]{2,1,0:T(1,128)S(1)}, f32[32,1,1024]{2,1,0:T(1,128)S(1)}, u32[]{:S(2)}, u32[]{:S(2)}) collective-permute-start(f32[32,1,1024]{2,1,0:T(1,128)S(1)} %get-tuple-element.19), channel_id=1, source_target_pairs={{0,8},{8,16},{16,24},{1,9},{9,17},{17,25},{2,10},{10,18},{18,26},{... | collective-permute-start | bytes 393224 | tf_op jit(solution)/shard_map/ppermute | solution.py:314
  9.7 30.3 %collective-permute-start.1 = (f32[1,64,1024]{2,1,0:T(8,128)S(1)}, f32[1,64,1024]{2,1,0:T(8,128)S(1)}, u32[]{:S(2)}, u32[]{:S(2)}) collective-permute-start(f32[1,64,1024]{2,1,0:T(8,128)S(1)} %get-tuple-element.20), channel_id=1, source_target_pairs={{1,0},{2,1},{3,2},{4,3},{5,4},{6,5},{7,6},{9,8},{10,9},{11,10},{12... | collective-permute-start | bytes 786440 | tf_op jit(solution)/shard_map/ppermute | solution.py:317
  11.0 29.0 %collective-permute-start = (f32[1,64,1024]{2,1,0:T(8,128)S(1)}, f32[1,64,1024]{2,1,0:T(8,128)S(1)}, u32[]{:S(2)}, u32[]{:S(2)}) collective-permute-start(f32[1,64,1024]{2,1,0:T(8,128)S(1)} %get-tuple-element.21), channel_id=1, source_target_pairs={{0,1},{1,2},{2,3},{3,4},{4,5},{5,6},{6,7},{8,9},{9,10},{10,11},{11... | collective-permute-start | bytes 786440 | tf_op jit(solution)/shard_map/ppermute | solution.py:316
  39.9 0.7 copy-start.2
  39.9 0.7 copy-start.3
  39.9 0.8 copy-start
  39.9 0.8 copy-start.1

commit v2 on v1

--- a/solution.py
+++ b/solution.py
@@ -10,7 +10,7 @@
 WEIGHT = 0.5
 STEP = 1000.0
 MESH = pl.DeviceIdType.MESH
-VMEM_LIMIT = 60 * 1024 * 1024
+VMEM_LIMIT = 24 * 1024 * 1024
 
 
 def shifted(a, by, fill):
@@ -43,19 +43,101 @@
     return p00 / p10
 
 
-def ladder_kernel(faces_ref, out_ref):
-    here = WEIGHT * STEP * faces_ref[...]
+def as_column(line, rows):
+    n = line.shape[1]
+    return jnp.transpose(jnp.broadcast_to(line, (n, n)))[:rows, :rows]
+
+
+def block_of_inverse(diagonal, sums, n):
+    i = lax.broadcasted_iota(jnp.int32, (n, n), 0)
+    j = lax.broadcasted_iota(jnp.int32, (n, n), 1)
+    near = jnp.where(i >= j, diagonal[:, :n], as_column(diagonal, n))
+    return near * jnp.exp(-jnp.abs(as_column(sums, n) - sums[:, :n]))
+
+
+def table_kernel(
+    nr, zc, yc, pos_ref, faces_ref, field_ref, xh_ref, xl_ref, xp_ref, ym_ref, yt_ref, zt_ref,
+    held_ref, sem,
+):
+    fetch = pltpu.make_async_copy(field_ref, held_ref, sem)
+    fetch.start()
+    row, col = pos_ref[0], pos_ref[1]
+    faces = faces_ref[...]
+    length = faces.shape[1]
+    nb, bx = xh_ref.shape[0], xh_ref.shape[1]
+    nx = nb * bx
+    here = WEIGHT * STEP * faces
     above = shifted(here, -1, 0.0)
     e = ladder(here, 1)
     h = ladder(above, -1)
     pivot = above + e
-    up = here / (here + h)
     down = above / pivot
-    out_ref[0:8] = 1.0 / (e + h - 1.0)
-    out_ref[8:16] = running_sum(jnp.log(jnp.maximum(up, 1e-30)))
-    out_ref[16:24] = running_sum(jnp.log(jnp.maximum(down, 1e-30)))
-    out_ref[24:32] = 1.0 / pivot
-    out_ref[32:40] = down
+    inverse = 1.0 / pivot
+    diag = 1.0 / (e + h - 1.0)
+    ups = running_sum(jnp.log(jnp.maximum(here / (here + h), 1e-30)))
+    downs = running_sum(jnp.log(jnp.maximum(down, 1e-30)))
+    ups_before, downs_before = shifted(ups, 1, 0.0), shifted(downs, 1, 0.0)
+    next_faces = shifted(faces, -1, 0.0)
+
+    xp_ref[2:3] = faces[0:1, :nx]
+    xp_ref[3:4] = next_faces[0:1, :nx]
+    for b in range(nb):
+        first, last = b * bx, (b + 1) * bx - 1
+        cols = slice(first, last + 1)
+        high, low = split(block_of_inverse(diag[0:1, cols], ups[0:1, cols], bx))
+        xh_ref[b] = high
+        xl_ref[b] = low
+        xp_ref[0:1, cols] = jnp.exp(ups[0:1, cols] - ups_before[0:1, first:first + 1])
+        xp_ref[1:2, cols] = jnp.exp(downs[0:1, last:last + 1] - downs_before[0:1, cols])
+
+    def own(values, which, start):
+        shift = lax.rem(length - start, length)
+        return pltpu.roll(values, shift, 1)[which:which + 1]
+
+    def passes(which, start, count):
+        u0, d0 = own(ups_before, which, start)[:, 0:1], own(downs_before, which, start)
+        u1, d1 = own(ups, which, start), own(downs, which, start)[:, count - 1:count]
+        return u1, u0, d1, jnp.exp(jnp.minimum(u1 - u0, 0.0)), jnp.exp(jnp.minimum(d1 - d0, 0.0))
+
+    wide = -(-yc // 128) * 128
+    y0 = row * yc
+    sums, up_first, down_last, onward, backward = passes(1, y0, yc)
+    block = block_of_inverse(own(diag, 1, y0)[:, :wide], sums[:, :wide], wide)[:yc, :yc]
+    high = block.astype(jnp.bfloat16).astype(jnp.float32)
+    ym_ref[:, 0:yc] = high
+    ym_ref[:, yc:2 * yc] = high
+    ym_ref[:, 2 * yc:3 * yc] = block - high
+    lines = [onward, backward, own(faces, 1, y0), own(next_faces, 1, y0)]
+    lines = [a[:, :wide] for a in lines] + [jnp.zeros((124, wide), jnp.float32)]
+    yt_ref[...] = jnp.transpose(jnp.concatenate(lines, axis=0))[:yc]
+
+    lane = lax.broadcasted_iota(jnp.int32, (1, 128), 1)
+    low_weights = high_weights = jnp.zeros((1, 128), jnp.float32)
+    for other in range(nr):
+        last, first = (other + 1) * yc - 1, other * yc
+        value = jnp.exp(jnp.minimum(up_first - ups[1:2, last:last + 1], 0.0))
+        low_weights = jnp.where(lane == other, value, low_weights)
+        value = jnp.exp(jnp.minimum(downs_before[1:2, first:first + 1] - down_last, 0.0))
+        high_weights = jnp.where(lane == other, value, high_weights)
+
+    z0 = col * zc
+    _, _, _, onward, backward = passes(2, z0, zc)
+    at = lax.broadcasted_iota(jnp.int32, (1, length), 1)
+    over = jnp.where(at == zc - 1, own(diag, 2, z0), own(inverse, 2, z0))
+    into = jnp.where(at == 0, 0.0, own(here, 2, z0) * over)
+    lines = [
+        over, into, own(down, 2, z0), own(faces, 2, z0), own(next_faces, 2, z0), onward, backward,
+    ]
+    for k, line in enumerate(lines):
+        zt_ref[k:k + 1] = line[:, :128]
+    zt_ref[7:8] = low_weights
+    zt_ref[8:9] = high_weights
+    zt_ref[9:16] = jnp.zeros((7, 128), jnp.float32)
+    fetch.wait()
+
+
+def on_chip(*shape):
+    return pltpu.VMEM(shape, jnp.float32)
 
 
 def split(a):
@@ -68,15 +150,14 @@
 
 
 def sweep_kernel(
-    planes, zco_ref, kz_ref, u_ref, before_ref, after_ref, zlo_ref, zhi_ref, ylo_ref, yhi_ref,
-    rea_ref, kx_ref, ky_ref, xh_ref, xl_ref, xp_ref, ym_ref, v_ref, ye_ref, ze_ref,
+    planes, zt_ref, u_ref, zlo_ref, zhi_ref, ylo_ref, yhi_ref,
+    rea_ref, yt_ref, xh_ref, xl_ref, xp_ref, ym_ref, v_ref, ye_ref, ze_ref,
 ):
     step, steps = pl.program_id(0), pl.num_programs(0)
-    _, yc, nx = u_ref.shape
-    zc = v_ref.shape[0]
+    zc, yc, nx = u_ref.shape
     nb, bx = xh_ref.shape[0], xh_ref.shape[1]
-    kx, kxn = kx_ref[0:1], kx_ref[1:2]
-    ky, kyn = ky_ref[:, 0:1], ky_ref[:, 1:2]
+    kx, kxn = xp_ref[2:3], xp_ref[3:4]
+    ky, kyn = yt_ref[:, 2:3], yt_ref[:, 3:4]
     lane = lax.broadcasted_iota(jnp.int32, (yc, nx), 1)
     sub = lax.broadcasted_iota(jnp.int32, (yc, nx), 0)
 
@@ -84,20 +165,21 @@
     def _():
         v_ref[0] = jnp.zeros((yc, nx), jnp.float32)
 
-    below = jnp.where(step == 0, zlo_ref[0], before_ref[0])
-    above_last = jnp.where(step == steps - 1, zhi_ref[0], after_ref[0])
+    below = jnp.where(step == 0, zlo_ref[0], u_ref[jnp.maximum(step * planes - 1, 0)])
+    above_last = u_ref[jnp.minimum((step + 1) * planes, zc - 1)]
+    above_last = jnp.where(step == steps - 1, zhi_ref[0], above_last)
     changes = []
     for p in range(planes):
         z = step * planes + p
-        u = u_ref[p]
-        above = u_ref[p + 1] if p + 1 < planes else above_last
+        u = u_ref[z]
+        above = u_ref[z + 1] if p + 1 < planes else above_last
         left = jnp.where(lane == 0, 0.0, pltpu.roll(u, 1, 1))
         right = pltpu.roll(u, nx - 1, 1)
         down = jnp.where(sub == 0, ylo_ref[p], pltpu.roll(u, 1, 0))
         upper = jnp.where(sub == yc - 1, yhi_ref[p], pltpu.roll(u, yc - 1, 0))
         total = kxn * (right - u) - kx * (u - left)
         total += kyn * (upper - u) - ky * (u - down)
-        total += kz_ref[1, z] * (above - u) - kz_ref[0, z] * (u - below)
+        total += zt_ref[4, z] * (above - u) - zt_ref[3, z] * (u - below)
         total += rea_ref[p] * u * (1.0 - u * u)
         changes.append(STEP * total)
         below = u
@@ -129,8 +211,8 @@
     for p in range(planes):
         z = step * planes + p
         high, low = split(solved[p * yc:(p + 1) * yc])
-        w = dot(ym_ref[...], jnp.concatenate([high, low, high], axis=0))
-        carry = zco_ref[0, z] * w + zco_ref[1, z] * carry
+        w = dot(ym_ref[...].astype(jnp.bfloat16), jnp.concatenate([high, low, high], axis=0))
+        carry = zt_ref[0, z] * w + zt_ref[1, z] * carry
         v_ref[z] = carry
 
     @pl.when(step == steps - 1)
@@ -145,7 +227,7 @@
 
             def back(i, value):
                 z = zc - 2 - i
-                value = v_ref[z, :, cols] + zco_ref[2, z] * value
+                value = v_ref[z, :, cols] + zt_ref[2, z] * value
                 v_ref[z, :, cols] = value
                 ye_ref[0, pl.ds(z, 1), cols] = value[0:1]
                 ye_ref[1, pl.ds(z, 1), cols] = value[yc - 1:yc]
@@ -155,7 +237,7 @@
 
 
 def exchange_kernel(
-    nr, nc, chunks, yw_ref, zw_ref, yp_ref, ye_ref, ze_ref, sy_ref, sz_ref,
+    nr, nc, chunks, zt_ref, yp_ref, ye_ref, ze_ref, sy_ref, sz_ref,
     ybuf, zbuf, zsend, ysend_sem, yrecv_sem, zsend_sem, zrecv_sem,
 ):
     row, col = lax.axis_index("row"), lax.axis_index("col")
@@ -202,12 +284,12 @@
         @pl.when(other < row)
         def _():
             y_copy(0, other, other).wait_recv()
-            sy_ref[0] += yw_ref[0, other] * ybuf[0, other]
+            sy_ref[0] += zt_ref[7, other] * ybuf[0, other]
 
         @pl.when(other > row)
         def _():
             y_copy(1, other, other).wait_recv()
-            sy_ref[1] += yw_ref[1, other] * ybuf[1, other]
+            sy_ref[1] += zt_ref[8, other] * ybuf[1, other]
 
     yb, ya = yp_ref[:, 0:1], yp_ref[:, 1:2]
     part = yc // chunks
@@ -226,6 +308,7 @@
     def scan(side):
         source, target = (has_low, has_high) if side == 0 else (has_high, has_low)
         edge, z = (1, zc - 1) if side == 0 else (0, 0)
+        through = zt_ref[5 + side, z]
         for k in range(chunks):
             rows = slice(k * part, (k + 1) * part)
 
@@ -242,7 +325,7 @@
             def _():
                 value = ze_ref[edge, rows] + yb[rows] * sy_ref[0, z:z + 1]
                 value += ya[rows] * sy_ref[1, z:z + 1]
-                zsend[side, rows] = value + zw_ref[side] * sz_ref[side, rows]
+                zsend[side, rows] = value + through * sz_ref[side, rows]
                 z_copy(side, k).start()
 
     low_half = col < nc // 2
@@ -276,26 +359,13 @@
             y_copy(1, other, row).wait_send()
 
 
-def finish_kernel(planes, zp_ref, u_ref, v_ref, yp_ref, sy_ref, sz_ref, out_ref):
+def finish_kernel(planes, zt_ref, u_ref, v_ref, yp_ref, sy_ref, sz_ref, out_ref):
     yb, ya = yp_ref[:, 0:1], yp_ref[:, 1:2]
     for p in range(planes):
         z = pl.program_id(0) * planes + p
-        value = u_ref[p] + v_ref[p]
+        value = u_ref[z] + v_ref[z]
         value += yb * sy_ref[0, pl.ds(z, 1)] + ya * sy_ref[1, pl.ds(z, 1)]
-        out_ref[p] = value + zp_ref[0, z] * sz_ref[0] + zp_ref[1, z] * sz_ref[1]
-
-
-def blocks_of_inverse(diagonal, sums):
-    n = diagonal.shape[-1]
-    i = lax.broadcasted_iota(jnp.int32, (n, n), 0)
-    j = lax.broadcasted_iota(jnp.int32, (n, n), 1)
-    near = jnp.where(i >= j, diagonal[..., None, :], diagonal[..., :, None])
-    return near * jnp.exp(-jnp.abs(sums[..., :, None] - sums[..., None, :]))
-
-
-def halves(a):
-    high = lax.reduce_precision(a, 8, 7)
-    return high.astype(jnp.bfloat16), (a - high).astype(jnp.bfloat16)
+        out_ref[p] = value + zt_ref[5, z] * sz_ref[0] + zt_ref[6, z] * sz_ref[1]
 
 
 def body(u, reaction, x_faces, y_faces, z_faces, x_inverse, y_inverse, z_inverse):
@@ -319,59 +389,32 @@
     longest = -(-max(nx, ny, nz) // 128) * 128
     faces = jnp.stack([jnp.pad(f, (0, longest - f.shape[0])) for f in (x_faces, y_faces, z_faces)])
     faces = jnp.pad(faces, ((0, 5), (0, 0)))
-    tables = pl.pallas_call(
-        ladder_kernel, out_shape=jax.ShapeDtypeStruct((40, longest), f32)
-    )(faces).reshape(5, 8, longest)
-
+    pos = jnp.stack([row, col]).astype(jnp.int32)
     bx = 256 if nx % 256 == 0 else nx
     nb = nx // bx
-    diag, up_sum, down_sum = (tables[i, 0, :nx].reshape(nb, bx) for i in range(3))
-    xh, xl = halves(blocks_of_inverse(diag, up_sum))
-    zero = jnp.zeros((1,), f32)
-    up_start = jnp.concatenate([zero, up_sum[:-1, -1]])[:, None]
-    down_before = jnp.concatenate([zero, tables[2, 0, :nx - 1]]).reshape(nb, bx)
-    xp = jnp.stack([jnp.exp(up_sum - up_start), jnp.exp(down_sum[:, -1:] - down_before)])
-    xp = xp.reshape(2, nx)
-    kx = jnp.stack([x_faces, jnp.concatenate([x_faces[1:], zero])])
-
-    def own(values, start, count):
-        return lax.dynamic_slice_in_dim(values, start, count)
-
-    def passes(which, n, start, count):
-        ups = jnp.concatenate([zero, tables[1, which, :n]])
-        downs = jnp.concatenate([zero, tables[2, which, :n]])
-        ups_here, downs_here = own(ups, start, count + 1), own(downs, start, count + 1)
-        onward = jnp.exp(ups_here[1:] - ups_here[0])
-        backward = jnp.exp(downs_here[count] - downs_here[:count])
-        return ups, downs, ups_here, downs_here, onward, backward
-
-    y0 = row * yc
-    ups, downs, ups_here, downs_here, onward, backward = passes(1, ny, y0, yc)
-    yh, yl = halves(blocks_of_inverse(own(tables[0, 1, :ny], y0, yc), ups_here[1:]))
-    ym = jnp.concatenate([yh, yh, yl], axis=1)
-    yp = jnp.stack([onward, backward], axis=1)
-    who = jnp.arange(nr)
-    from_low = jnp.where(who < row, jnp.exp(jnp.minimum(ups_here[0] - ups[yc::yc], 0.0)), 0.0)
-    from_high = jnp.where(who > row, jnp.exp(jnp.minimum(downs[:-1:yc] - downs_here[yc], 0.0)), 0.0)
-    yw = jnp.stack([from_low, from_high])
-    yf = jnp.concatenate([y_faces, zero])
-    ky = jnp.stack([own(yf, y0, yc), own(yf, y0 + 1, yc)], axis=1)
-
-    z0 = col * zc
-    _, _, _, _, z_onward, z_backward = passes(2, nz, z0, zc)
-    zp = jnp.stack([z_onward, z_backward])
-    zw = jnp.stack([z_onward[-1], z_backward[0]])
-    zf = jnp.concatenate([z_faces, zero])
-    kz = jnp.stack([own(zf, z0, zc), own(zf, z0 + 1, zc)])
-    at = jnp.arange(zc)
-    over = jnp.where(at == zc - 1, own(tables[0, 2, :nz], z0, zc), own(tables[3, 2, :nz], z0, zc))
-    into = jnp.where(at == 0, 0.0, WEIGHT * STEP * kz[0] * over)
-    zco = jnp.stack([over, into, own(tables[4, 2, :nz], z0, zc)])
+    smem = pl.BlockSpec(memory_space=pltpu.SMEM)
+    vmem = pl.BlockSpec(memory_space=pltpu.VMEM)
+    xh, xl, xp, ym, yt, zt, held = pl.pallas_call(
+        functools.partial(table_kernel, nr, zc, yc),
+        in_specs=[smem, vmem, pl.BlockSpec(memory_space=pltpu.HBM)],
+        out_specs=[vmem] * 7,
+        out_shape=[
+            jax.ShapeDtypeStruct((nb, bx, bx), jnp.bfloat16),
+            jax.ShapeDtypeStruct((nb, bx, bx), jnp.bfloat16),
+            jax.ShapeDtypeStruct((4, nx), f32),
+            jax.ShapeDtypeStruct((yc, 3 * yc), f32),
+            jax.ShapeDtypeStruct((yc, 128), f32),
+            jax.ShapeDtypeStruct((16, 128), f32),
+            on_chip(zc, yc, nx),
+        ],
+        scratch_shapes=[pltpu.SemaphoreType.DMA(())],
+        compiler_params=pltpu.CompilerParams(vmem_limit_bytes=VMEM_LIMIT),
+        cost_estimate=pl.CostEstimate(flops=40000000, bytes_accessed=1 << 20, transcendentals=0),
+    )(pos, faces, u)
 
     planes = 2 if zc % 2 == 0 else 1
     steps = zc // planes
-    smem = pl.BlockSpec(memory_space=pltpu.SMEM)
-    vmem = pl.BlockSpec(memory_space=pltpu.VMEM)
+    reaction = pltpu.with_memory_space_constraint(reaction, pltpu.HBM)
     plane = (1, yc, nx)
 
     def whole(*shape):
@@ -383,26 +426,22 @@
         functools.partial(sweep_kernel, planes),
         grid=(steps,),
         in_specs=[
-            smem, smem, slab,
-            pl.BlockSpec(plane, lambda s: (jnp.maximum(s * planes - 1, 0), 0, 0)),
-            pl.BlockSpec(plane, lambda s: (jnp.minimum((s + 1) * planes, zc - 1), 0, 0)),
-            whole(*plane), whole(*plane), line, line, slab,
-            whole(2, nx), whole(yc, 2), whole(nb, bx, bx), whole(nb, bx, bx), whole(2, nx),
-            whole(yc, 3 * yc),
-        ],
-        out_specs=[whole(zc, yc, nx), whole(2, zc, nx), whole(2, yc, nx)],
+            smem, vmem, whole(*plane), whole(*plane), line, line, slab,
+            whole(yc, 128), whole(nb, bx, bx), whole(nb, bx, bx), whole(4, nx), whole(yc, 3 * yc),
+        ],
+        out_specs=[vmem, whole(2, zc, nx), whole(2, yc, nx)],
         out_shape=[
-            jax.ShapeDtypeStruct((zc, yc, nx), f32),
+            on_chip(zc, yc, nx),
             jax.ShapeDtypeStruct((2, zc, nx), f32),
             jax.ShapeDtypeStruct((2, yc, nx), f32),
         ],
         compiler_params=pltpu.CompilerParams(vmem_limit_bytes=VMEM_LIMIT),
-    )(zco, kz, u, u, u, zlo, zhi, ylo, yhi, reaction, kx, ky, xh, xl, xp, ym)
+    )(zt, held, zlo, zhi, ylo, yhi, reaction, yt, xh, xl, xp, ym)
 
     chunks = 4 if yc % 32 == 0 else 1
     sy, sz = pl.pallas_call(
         functools.partial(exchange_kernel, nr, nc, chunks),
-        in_specs=[smem, smem, vmem, vmem, vmem],
+        in_specs=[smem, vmem, vmem, vmem],
         out_specs=[vmem, vmem],
         out_shape=[
             jax.ShapeDtypeStruct((2, zc, nx), f32),
@@ -420,16 +459,16 @@
         compiler_params=pltpu.CompilerParams(
             collective_id=0, has_side_effects=True, vmem_limit_bytes=VMEM_LIMIT
         ),
-    )(yw, zw, yp, ye, ze)
+    )(zt, yt, ye, ze)
 
     return pl.pallas_call(
         functools.partial(finish_kernel, planes),
         grid=(steps,),
-        in_specs=[smem, slab, slab, whole(yc, 2), whole(2, zc, nx), whole(2, yc, nx)],
+        in_specs=[smem, vmem, vmem, whole(yc, 128), whole(2, zc, nx), whole(2, yc, nx)],
         out_specs=slab,
         out_shape=jax.ShapeDtypeStruct((zc, yc, nx), f32),
         compiler_params=pltpu.CompilerParams(vmem_limit_bytes=VMEM_LIMIT),
-    )(zp, u, v, yp, sy, sz)
+    )(zt, held, v, yt, sy, sz)
 
 
 def solution(mesh):

time: 116 us -> 84.3 us (0.73); the launches traced: 114 us -> 84 us
  other arithmetic: 14 us -> 0.78 us
  Pallas kernels: 76.5 us -> 64.4 us
  local copies, waits for them, and re-layouts: 12.7 us -> 7.57 us
    another operation x16 -> x1, other arithmetic: 7.8 us -> 0.08 us  [body(): pos = jnp.stack([row, col]).astype(jnp.int32)]
    pallas_call x1, Pallas kernels: 15.3 us -> 9.26 us  [body(): pl.pallas_call(functools.partial(finish_kernel, planes), grid=(steps,), i...]
    slice x10 -> x0, local copies, waits for them, and re-layouts: 4.57 us -> none  [the longest x2 1.24 us: passes(): backward = jnp.exp(downs_here[count] - downs_here[:count])]
    pallas_call x1, Pallas kernels: 29.4 us -> 25 us  [body(): pl.pallas_call(functools.partial(sweep_kernel, planes), grid=(steps,), in...]
    pallas_call x1, Pallas kernels: 28.9 us -> 26.7 us  [body(): pl.pallas_call(functools.partial(exchange_kernel, nr, nc, chunks), in_spe...]
    unnamed x14 -> x2, local copies, waits for them, and re-layouts: 1.19 us -> 3.38 us
    concatenate x6 -> x0, other arithmetic: 1.7 us -> none  [the longest x1 0.71 us: body(): yf = jnp.concatenate([y_faces, zero])]
    exp x3 -> x0, other arithmetic: 1.59 us -> none  [the longest x1 0.84 us: body(): jnp.exp(down_sum[:, -1:] - down_before)]
  transfers between devices with their start and end apart: 4 -> 4, of which waited for: 0 -> 0; matrix products, arithmetic and copies ran while one was open for 21% -> 5% of each run, Pallas kernels for 2% -> 4%
where the time goes in v2:
time: 84.3 us; the launch traced here: 84 us
  Pallas kernels  64.4 us (76%)
  starting transfers between devices  11.1 us (13%)
  local copies, waits for them, and re-layouts  7.57 us (9%)
    pallas_call x1, Pallas kernels, body(): pl.pallas_call(functools.partial(exchange_kernel, nr, nc, chunks), in_spe...  26.7 us
    pallas_call x1, Pallas kernels, body(): pl.pallas_call(functools.partial(sweep_kernel, planes), grid=(steps,), in...  25 us
    pallas_call x1, Pallas kernels, body(): pl.pallas_call(functools.partial(finish_kernel, planes), grid=(steps,), i...  9.26 us
    ppermute x1, starting transfers between devices, body(): ylo = lax.ppermute(u[:, yc - 1:yc], 'row', up(nr))  5.51 us
    pallas_call x1, Pallas kernels, body(): pl.pallas_call(functools.partial(table_kernel, nr, zc, yc), in_specs=[sme...  3.4 us
    unnamed x2, local copies, waits for them, and re-layouts  3.38 us
    ppermute x1, starting transfers between devices, body(): zlo = lax.ppermute(u[zc - 1:zc], 'col', up(nc))  3.05 us
    slice x1, local copies, waits for them, and re-layouts, body(): yhi = lax.ppermute(u[:, 0:1], 'row', down(nr))  1.76 us
  transfers between devices with their start and end apart: 4, of which 0 were waited for; matrix products, arithmetic and copies ran while one was open for 5% of the time, Pallas kernels for 4%

profile of v2, /device:TPU:0, one launch (start us, length us, event | category | flops | bytes accessed | tf_op | source)
XLA Modules:
  0.0 84.0 jit_solution(13332129569642225805)
XLA Ops:
  0.0 1.1 %fusion.1 = (f32[1,64,1024]{2,1,0:T(8,128)S(1)}, f32[1,64,1024]{2,1,0:T(8,128)S(1)}) fusion(f32[32,64,1024]{2,1,0:T(8,128)} %field_ref.1), kind=kLoop, calls=%fused_computation.5 | loop fusion | bytes 1048576 | tf_op jit(solution)/shard_map/slice | solution.py:387
  1.1 1.3 %collective-permute-start.1 = (f32[1,64,1024]{2,1,0:T(8,128)S(1)}, f32[1,64,1024]{2,1,0:T(8,128)S(1)}, u32[]{:S(2)}, u32[]{:S(2)}) collective-permute-start(f32[1,64,1024]{2,1,0:T(8,128)S(1)} %get-tuple-element.31), channel_id=1, source_target_pairs={{1,0},{2,1},{3,2},{4,3},{5,4},{6,5},{7,6},{9,8},{10,9},{11,10},{12... | collective-permute-start | bytes 786440 | tf_op jit(solution)/shard_map/ppermute | solution.py:387
  2.4 3.0 %collective-permute-start = (f32[1,64,1024]{2,1,0:T(8,128)S(1)}, f32[1,64,1024]{2,1,0:T(8,128)S(1)}, u32[]{:S(2)}, u32[]{:S(2)}) collective-permute-start(f32[1,64,1024]{2,1,0:T(8,128)S(1)} %get-tuple-element.32), channel_id=1, source_target_pairs={{0,1},{1,2},{2,3},{3,4},{4,5},{5,6},{6,7},{8,9},{9,10},{10,11},{11... | collective-permute-start | bytes 786440 | tf_op jit(solution)/shard_map/ppermute | solution.py:386
  5.4 1.8 %fusion = (f32[32,1,1024]{2,1,0:T(1,128)S(1)}, f32[32,1,1024]{2,1,0:T(1,128)S(1)}) fusion(f32[32,64,1024]{2,1,0:T(8,128)} %field_ref.1), kind=kLoop, calls=%fused_computation.4 | loop fusion | bytes 524288 | tf_op jit(solution)/shard_map/slice | solution.py:385
  7.2 1.3 %collective-permute-start.3 = (f32[32,1,1024]{2,1,0:T(1,128)S(1)}, f32[32,1,1024]{2,1,0:T(1,128)S(1)}, u32[]{:S(2)}, u32[]{:S(2)}) collective-permute-start(f32[32,1,1024]{2,1,0:T(1,128)S(1)} %get-tuple-element.29), channel_id=1, source_target_pairs={{8,0},{16,8},{24,16},{9,1},{17,9},{25,17},{10,2},{18,10},{26,18},{... | collective-permute-start | bytes 393224 | tf_op jit(solution)/shard_map/ppermute | solution.py:385
  8.5 5.5 %collective-permute-start.2 = (f32[32,1,1024]{2,1,0:T(1,128)S(1)}, f32[32,1,1024]{2,1,0:T(1,128)S(1)}, u32[]{:S(2)}, u32[]{:S(2)}) collective-permute-start(f32[32,1,1024]{2,1,0:T(1,128)S(1)} %get-tuple-element.30), channel_id=1, source_target_pairs={{0,8},{8,16},{16,24},{1,9},{9,17},{17,25},{2,10},{10,18},{18,26},{... | collective-permute-start | bytes 393224 | tf_op jit(solution)/shard_map/ppermute | solution.py:384
  14.0 0.1 pad_add_fusion.pos_ref
  14.1 0.7 pad.11
  14.8 0.7 pad.12
  15.5 0.7 select_maximum_fusion.faces_ref
  16.2 0.0 copy-start
  16.2 3.4 %copy-done = f32[32,64,1024]{2,1,0:T(8,128)S(1)} copy-done((f32[32,64,1024]{2,1,0:T(8,128)S(1)}, f32[32,64,1024]{2,1,0:T(8,128)}, u32[]{:S(2)}) %copy-start) | copy-done | bytes 8388632
  19.5 3.4 %shard_map.55 = (bf16[4,256,256]{2,1,0:T(8,128)(2,1)S(1)}, bf16[4,256,256]{2,1,0:T(8,128)(2,1)S(1)}, f32[4,1024]{1,0:T(4,128)S(1)}, f32[64,192]{1,0:T(8,128)S(1)...) custom-call(s32[2]{0:T(128)S(1)} %pad_add_fusion.pos_ref, ...), custom_call_target="tpu_custom_call" | custom-call | flops 40000000 | bytes 1048576 | tf_op jit(solution)/shard_map/pallas_call | solution.py:397
  23.0 0.0 collective-permute-done.3.yhi_ref
  23.0 0.0 collective-permute-done.2.ylo_ref
  23.0 0.0 collective-permute-done.1.zhi_ref
  23.0 0.0 collective-permute-done.zlo_ref
  23.0 25.0 %shard_map.56 = (f32[32,64,1024]{2,1,0:T(8,128)S(1)}, f32[2,32,1024]{2,1,0:T(8,128)S(1)}, f32[2,64,1024]{2,1,0:T(8,128)S(1)}) custom-call(f32[16,128]{1,0:T(8,128)S(1)} %get-tuple-element.17.zt_ref, f32[32,64,1024]{2,1,0:T(8,128)S(1)} %get-tuple-element.18.u_ref, f32[1,64,1024]{2,1,0:T(8,128)S(1)} %collective-permute-done.zlo_ref, ...), custom_call_target="tpu_custom_call" | custom-call | tf_op jit(solution)/shard_map/pallas_call | solution.py:425
  48.0 26.7 %shard_map.57 = (f32[2,32,1024]{2,1,0:T(8,128)S(1)}, f32[2,64,1024]{2,1,0:T(8,128)S(1)}) custom-call(f32[16,128]{1,0:T(8,128)S(1)} %get-tuple-element.17.zt_ref, f32[64,128]{1,0:T(8,128)S(1)} %get-tuple-element.19.yt_ref.yp_ref, f32[2,32,1024]{2,1,0:T(8,128)S(1)} %get-tuple-element.25.ye_ref, f32[2,64,1024]{2,1,0:T(8,128)S(1)} %get-tuple-element.26.ze_ref), custom_call_target="tpu_custom_call" | custom-call | tf_op jit(solution)/shard_map/pallas_call | solution.py:442
  74.7 9.3 %shard_map.58 = f32[32,64,1024]{2,1,0:T(8,128)} custom-call(f32[16,128]{1,0:T(8,128)S(1)} %get-tuple-element.17.zt_ref, f32[32,64,1024]{2,1,0:T(8,128)S(1)} %get-tuple-element.18.u_ref, f32[32,64,1024]{2,1,0:T(8,128)S(1)} %get-tuple-element.24.v_ref, f32[64,128]{1,0:T(8,128)S(1)} %get-tuple-element.19.yt_ref.yp_ref, ...), custom_call_target="tpu_custom_call" | custom-call | tf_op jit(solution)/shard_map/pallas_call | solution.py:464
Async XLA Ops:
  1.1 21.9 %collective-permute-start.1 = (f32[1,64,1024]{2,1,0:T(8,128)S(1)}, f32[1,64,1024]{2,1,0:T(8,128)S(1)}, u32[]{:S(2)}, u32[]{:S(2)}) collective-permute-start(f32[1,64,1024]{2,1,0:T(8,128)S(1)} %get-tuple-element.31), channel_id=1, source_target_pairs={{1,0},{2,1},{3,2},{4,3},{5,4},{6,5},{7,6},{9,8},{10,9},{11,10},{12... | collective-permute-start | bytes 786440 | tf_op jit(solution)/shard_map/ppermute | solution.py:387
  2.4 20.6 %collective-permute-start = (f32[1,64,1024]{2,1,0:T(8,128)S(1)}, f32[1,64,1024]{2,1,0:T(8,128)S(1)}, u32[]{:S(2)}, u32[]{:S(2)}) collective-permute-start(f32[1,64,1024]{2,1,0:T(8,128)S(1)} %get-tuple-element.32), channel_id=1, source_target_pairs={{0,1},{1,2},{2,3},{3,4},{4,5},{5,6},{6,7},{8,9},{9,10},{10,11},{11... | collective-permute-start | bytes 786440 | tf_op jit(solution)/shard_map/ppermute | solution.py:386
  7.2 15.8 %collective-permute-start.3 = (f32[32,1,1024]{2,1,0:T(1,128)S(1)}, f32[32,1,1024]{2,1,0:T(1,128)S(1)}, u32[]{:S(2)}, u32[]{:S(2)}) collective-permute-start(f32[32,1,1024]{2,1,0:T(1,128)S(1)} %get-tuple-element.29), channel_id=1, source_target_pairs={{8,0},{16,8},{24,16},{9,1},{17,9},{25,17},{10,2},{18,10},{26,18},{... | collective-permute-start | bytes 393224 | tf_op jit(solution)/shard_map/ppermute | solution.py:385
  8.5 14.5 %collective-permute-start.2 = (f32[32,1,1024]{2,1,0:T(1,128)S(1)}, f32[32,1,1024]{2,1,0:T(1,128)S(1)}, u32[]{:S(2)}, u32[]{:S(2)}) collective-permute-start(f32[32,1,1024]{2,1,0:T(1,128)S(1)} %get-tuple-element.30), channel_id=1, source_target_pairs={{0,8},{8,16},{16,24},{1,9},{9,17},{17,25},{2,10},{10,18},{18,26},{... | collective-permute-start | bytes 393224 | tf_op jit(solution)/shard_map/ppermute | solution.py:384
  16.2 3.4 %copy-start = (f32[32,64,1024]{2,1,0:T(8,128)S(1)}, f32[32,64,1024]{2,1,0:T(8,128)}, u32[]{:S(2)}) copy-start(f32[32,64,1024]{2,1,0:T(8,128)} %field_ref.1) | copy-start | bytes 25165828

commit v3 on v2

--- a/solution.py
+++ b/solution.py
@@ -56,12 +56,72 @@
 
 
 def table_kernel(
-    nr, zc, yc, pos_ref, faces_ref, field_ref, xh_ref, xl_ref, xp_ref, ym_ref, yt_ref, zt_ref,
-    held_ref, sem,
+    nr, nc, faces_ref, field_ref, xh_ref, xl_ref, xp_ref, ym_ref, yt_ref, zt_ref,
+    held_ref, yhalo_ref, zhalo_ref, strips, edges, fetch_sem, strip_sem, send_sem, recv_sem,
 ):
-    fetch = pltpu.make_async_copy(field_ref, held_ref, sem)
+    row, col = lax.axis_index("row"), lax.axis_index("col")
+    zc, yc, _ = field_ref.shape
+    tall = strips.shape[2]
+    strip_copies = [
+        pltpu.make_async_copy(
+            field_ref.at[:, pl.ds(start, tall)], strips.at[side], strip_sem.at[side]
+        )
+        for side, start in ((0, yc - tall), (1, 0))
+    ]
+    for copy in strip_copies:
+        copy.start()
+    fetch = pltpu.make_async_copy(field_ref, held_ref, fetch_sem)
     fetch.start()
-    row, col = pos_ref[0], pos_ref[1]
+    places = [
+        (row < nr - 1, row > 0, (row + 1, col)),
+        (row > 0, row < nr - 1, (row - 1, col)),
+        (col < nc - 1, col > 0, (row, col + 1)),
+        (col > 0, col < nc - 1, (row, col - 1)),
+    ]
+    barrier = pltpu.get_barrier_semaphore()
+    expected = 0
+    for to, _, device in places:
+        expected += to.astype(jnp.int32)
+
+        @pl.when(to)
+        def _():
+            pl.semaphore_signal(barrier, inc=1, device_id=device, device_id_type=MESH)
+
+    pl.semaphore_wait(barrier, expected)
+    ends = [
+        (edges.at[0], yhalo_ref.at[0]),
+        (edges.at[1], yhalo_ref.at[1]),
+        (field_ref.at[zc - 1], zhalo_ref.at[0]),
+        (field_ref.at[0], zhalo_ref.at[1]),
+    ]
+    halo = [
+        pltpu.make_async_remote_copy(
+            src_ref=source, dst_ref=target, send_sem=send_sem.at[k], recv_sem=recv_sem.at[k],
+            device_id=places[k][2], device_id_type=MESH,
+        )
+        for k, (source, target) in enumerate(ends)
+    ]
+    for k in (2, 3):
+        @pl.when(places[k][0])
+        def _():
+            halo[k].start()
+
+    for side in (0, 1):
+        strip_copies[side].wait()
+        for z in range(zc):
+            at = tall - 1 if side == 0 else 0
+            edges[side, z:z + 1] = strips[side, z, at:at + 1]
+
+        @pl.when(places[side][0])
+        def _():
+            halo[side].start()
+
+    for k in range(4):
+        @pl.when(jnp.logical_not(places[k][1]))
+        def _():
+            target = ends[k][1]
+            target[...] = jnp.zeros_like(target)
+
     faces = faces_ref[...]
     length = faces.shape[1]
     nb, bx = xh_ref.shape[0], xh_ref.shape[1]
@@ -133,6 +193,15 @@
     zt_ref[7:8] = low_weights
     zt_ref[8:9] = high_weights
     zt_ref[9:16] = jnp.zeros((7, 128), jnp.float32)
+    for k in range(4):
+        @pl.when(places[k][0])
+        def _():
+            halo[k].wait_send()
+
+        @pl.when(places[k][1])
+        def _():
+            halo[k].wait_recv()
+
     fetch.wait()
 
 
@@ -150,7 +219,7 @@
 
 
 def sweep_kernel(
-    planes, zt_ref, u_ref, zlo_ref, zhi_ref, ylo_ref, yhi_ref,
+    planes, zt_ref, u_ref, yhalo_ref, zhalo_ref,
     rea_ref, yt_ref, xh_ref, xl_ref, xp_ref, ym_ref, v_ref, ye_ref, ze_ref,
 ):
     step, steps = pl.program_id(0), pl.num_programs(0)
@@ -165,9 +234,9 @@
     def _():
         v_ref[0] = jnp.zeros((yc, nx), jnp.float32)
 
-    below = jnp.where(step == 0, zlo_ref[0], u_ref[jnp.maximum(step * planes - 1, 0)])
+    below = jnp.where(step == 0, zhalo_ref[0], u_ref[jnp.maximum(step * planes - 1, 0)])
     above_last = u_ref[jnp.minimum((step + 1) * planes, zc - 1)]
-    above_last = jnp.where(step == steps - 1, zhi_ref[0], above_last)
+    above_last = jnp.where(step == steps - 1, zhalo_ref[1], above_last)
     changes = []
     for p in range(planes):
         z = step * planes + p
@@ -175,8 +244,8 @@
         above = u_ref[z + 1] if p + 1 < planes else above_last
         left = jnp.where(lane == 0, 0.0, pltpu.roll(u, 1, 1))
         right = pltpu.roll(u, nx - 1, 1)
-        down = jnp.where(sub == 0, ylo_ref[p], pltpu.roll(u, 1, 0))
-        upper = jnp.where(sub == yc - 1, yhi_ref[p], pltpu.roll(u, yc - 1, 0))
+        down = jnp.where(sub == 0, yhalo_ref[0, pl.ds(z, 1)], pltpu.roll(u, 1, 0))
+        upper = jnp.where(sub == yc - 1, yhalo_ref[1, pl.ds(z, 1)], pltpu.roll(u, yc - 1, 0))
         total = kxn * (right - u) - kx * (u - left)
         total += kyn * (upper - u) - ky * (u - down)
         total += zt_ref[4, z] * (above - u) - zt_ref[3, z] * (u - below)
@@ -238,7 +307,8 @@
 
 def exchange_kernel(
     nr, nc, chunks, zt_ref, yp_ref, ye_ref, ze_ref, sy_ref, sz_ref,
-    ybuf, zbuf, zsend, ysend_sem, yrecv_sem, zsend_sem, zrecv_sem,
+    ybuf, zbuf, zsend, esend, ebuf, ysend_sem, yrecv_sem, zsend_sem, zrecv_sem,
+    esend_sem, erecv_sem,
 ):
     row, col = lax.axis_index("row"), lax.axis_index("col")
     zc, nx = ye_ref.shape[1], ye_ref.shape[2]
@@ -279,19 +349,6 @@
         def _():
             y_copy(1, other, row).start()
 
-    sy_ref[...] = jnp.zeros_like(sy_ref)
-    for other in range(nr):
-        @pl.when(other < row)
-        def _():
-            y_copy(0, other, other).wait_recv()
-            sy_ref[0] += zt_ref[7, other] * ybuf[0, other]
-
-        @pl.when(other > row)
-        def _():
-            y_copy(1, other, other).wait_recv()
-            sy_ref[1] += zt_ref[8, other] * ybuf[1, other]
-
-    yb, ya = yp_ref[:, 0:1], yp_ref[:, 1:2]
     part = yc // chunks
 
     def z_copy(side, k):
@@ -323,9 +380,7 @@
 
             @pl.when(target)
             def _():
-                value = ze_ref[edge, rows] + yb[rows] * sy_ref[0, z:z + 1]
-                value += ya[rows] * sy_ref[1, z:z + 1]
-                zsend[side, rows] = value + through * sz_ref[side, rows]
+                zsend[side, rows] = ze_ref[edge, rows] + through * sz_ref[side, rows]
                 z_copy(side, k).start()
 
     low_half = col < nc // 2
@@ -340,6 +395,50 @@
     def _():
         scan(0)
 
+    for k in range(2):
+        esend[0, k:k + 1] = sz_ref[k, yc - 1:yc]
+        esend[1, k:k + 1] = sz_ref[k, 0:1]
+
+    def e_copy(side, other, slot):
+        return pltpu.make_async_remote_copy(
+            src_ref=esend.at[side],
+            dst_ref=ebuf.at[side, slot],
+            send_sem=esend_sem.at[side, other],
+            recv_sem=erecv_sem.at[side, slot],
+            device_id=(other, col),
+            device_id_type=MESH,
+        )
+
+    for other in range(nr):
+        @pl.when(other > row)
+        def _():
+            e_copy(0, other, row).start()
+
+        @pl.when(other < row)
+        def _():
+            e_copy(1, other, row).start()
+
+    sy_ref[...] = jnp.zeros_like(sy_ref)
+    for other in range(nr):
+        @pl.when(other < row)
+        def _():
+            y_copy(0, other, other).wait_recv()
+            sy_ref[0] += zt_ref[7, other] * ybuf[0, other]
+
+        @pl.when(other > row)
+        def _():
+            y_copy(1, other, other).wait_recv()
+            sy_ref[1] += zt_ref[8, other] * ybuf[1, other]
+
+    for other in range(nr):
+        for side, here in ((0, other < row), (1, other > row)):
+            @pl.when(here)
+            def _():
+                e_copy(side, other, other).wait_recv()
+                coefficients = zt_ref[7 + side, other] * yp_ref[:, side:side + 1]
+                for k in range(2):
+                    sz_ref[k] += coefficients * ebuf[side, other, k:k + 1]
+
     for k in range(chunks):
         @pl.when(has_high)
         def _():
@@ -350,13 +449,11 @@
             z_copy(1, k).wait_send()
 
     for other in range(nr):
-        @pl.when(other > row)
-        def _():
-            y_copy(0, other, row).wait_send()
-
-        @pl.when(other < row)
-        def _():
-            y_copy(1, other, row).wait_send()
+        for side, there in ((0, other > row), (1, other < row)):
+            @pl.when(there)
+            def _():
+                y_copy(side, other, row).wait_send()
+                e_copy(side, other, row).wait_send()
 
 
 def finish_kernel(planes, zt_ref, u_ref, v_ref, yp_ref, sy_ref, sz_ref, out_ref):
@@ -371,33 +468,21 @@
 def body(u, reaction, x_faces, y_faces, z_faces, x_inverse, y_inverse, z_inverse):
     zc, yc, nx = u.shape
     nr, nc = lax.axis_size("row"), lax.axis_size("col")
-    row, col = lax.axis_index("row"), lax.axis_index("col")
     ny, nz = y_faces.shape[0], z_faces.shape[0]
     f32 = jnp.float32
-
-    def up(n):
-        return [(i, i + 1) for i in range(n - 1)]
-
-    def down(n):
-        return [(i + 1, i) for i in range(n - 1)]
-
-    ylo = lax.ppermute(u[:, yc - 1:yc], "row", up(nr))
-    yhi = lax.ppermute(u[:, 0:1], "row", down(nr))
-    zlo = lax.ppermute(u[zc - 1:zc], "col", up(nc))
-    zhi = lax.ppermute(u[0:1], "col", down(nc))
 
     longest = -(-max(nx, ny, nz) // 128) * 128
     faces = jnp.stack([jnp.pad(f, (0, longest - f.shape[0])) for f in (x_faces, y_faces, z_faces)])
     faces = jnp.pad(faces, ((0, 5), (0, 0)))
-    pos = jnp.stack([row, col]).astype(jnp.int32)
+    tall = 8 if yc % 8 == 0 else yc
     bx = 256 if nx % 256 == 0 else nx
     nb = nx // bx
     smem = pl.BlockSpec(memory_space=pltpu.SMEM)
     vmem = pl.BlockSpec(memory_space=pltpu.VMEM)
-    xh, xl, xp, ym, yt, zt, held = pl.pallas_call(
-        functools.partial(table_kernel, nr, zc, yc),
-        in_specs=[smem, vmem, pl.BlockSpec(memory_space=pltpu.HBM)],
-        out_specs=[vmem] * 7,
+    xh, xl, xp, ym, yt, zt, held, yhalo, zhalo = pl.pallas_call(
+        functools.partial(table_kernel, nr, nc),
+        in_specs=[vmem, pl.BlockSpec(memory_space=pltpu.HBM)],
+        out_specs=[vmem] * 9,
         out_shape=[
             jax.ShapeDtypeStruct((nb, bx, bx), jnp.bfloat16),
             jax.ShapeDtypeStruct((nb, bx, bx), jnp.bfloat16),
@@ -406,27 +491,36 @@
             jax.ShapeDtypeStruct((yc, 128), f32),
             jax.ShapeDtypeStruct((16, 128), f32),
             on_chip(zc, yc, nx),
-        ],
-        scratch_shapes=[pltpu.SemaphoreType.DMA(())],
-        compiler_params=pltpu.CompilerParams(vmem_limit_bytes=VMEM_LIMIT),
+            on_chip(2, zc, nx),
+            on_chip(2, yc, nx),
+        ],
+        scratch_shapes=[
+            pltpu.VMEM((2, zc, tall, nx), f32),
+            pltpu.VMEM((2, zc, nx), f32),
+            pltpu.SemaphoreType.DMA(()),
+            pltpu.SemaphoreType.DMA((2,)),
+            pltpu.SemaphoreType.DMA((4,)),
+            pltpu.SemaphoreType.DMA((4,)),
+        ],
+        compiler_params=pltpu.CompilerParams(
+            collective_id=1, has_side_effects=True, vmem_limit_bytes=VMEM_LIMIT
+        ),
         cost_estimate=pl.CostEstimate(flops=40000000, bytes_accessed=1 << 20, transcendentals=0),
-    )(pos, faces, u)
+    )(faces, pltpu.with_memory_space_constraint(u, pltpu.HBM))
 
     planes = 2 if zc % 2 == 0 else 1
     steps = zc // planes
     reaction = pltpu.with_memory_space_constraint(reaction, pltpu.HBM)
-    plane = (1, yc, nx)
 
     def whole(*shape):
         return pl.BlockSpec(shape, lambda s: (0,) * len(shape))
 
     slab = pl.BlockSpec((planes, yc, nx), lambda s: (s, 0, 0))
-    line = pl.BlockSpec((planes, 1, nx), lambda s: (s, 0, 0))
     v, ye, ze = pl.pallas_call(
         functools.partial(sweep_kernel, planes),
         grid=(steps,),
         in_specs=[
-            smem, vmem, whole(*plane), whole(*plane), line, line, slab,
+            smem, vmem, vmem, vmem, slab,
             whole(yc, 128), whole(nb, bx, bx), whole(nb, bx, bx), whole(4, nx), whole(yc, 3 * yc),
         ],
         out_specs=[vmem, whole(2, zc, nx), whole(2, yc, nx)],
@@ -436,9 +530,9 @@
             jax.ShapeDtypeStruct((2, yc, nx), f32),
         ],
         compiler_params=pltpu.CompilerParams(vmem_limit_bytes=VMEM_LIMIT),
-    )(zt, held, zlo, zhi, ylo, yhi, reaction, yt, xh, xl, xp, ym)
-
-    chunks = 4 if yc % 32 == 0 else 1
+    )(zt, held, yhalo, zhalo, reaction, yt, xh, xl, xp, ym)
+
+    chunks = yc // 8 if yc % 8 == 0 else 1
     sy, sz = pl.pallas_call(
         functools.partial(exchange_kernel, nr, nc, chunks),
         in_specs=[smem, vmem, vmem, vmem],
@@ -451,10 +545,14 @@
             pltpu.VMEM((2, nr, zc, nx), f32),
             pltpu.VMEM((2, yc, nx), f32),
             pltpu.VMEM((2, yc, nx), f32),
+            pltpu.VMEM((2, 2, nx), f32),
+            pltpu.VMEM((2, nr, 2, nx), f32),
             pltpu.SemaphoreType.DMA((2, nr)),
             pltpu.SemaphoreType.DMA((2, nr)),
             pltpu.SemaphoreType.DMA((2, chunks)),
             pltpu.SemaphoreType.DMA((2, chunks)),
+            pltpu.SemaphoreType.DMA((2, nr)),
+            pltpu.SemaphoreType.DMA((2, nr)),
         ],
         compiler_params=pltpu.CompilerParams(
             collective_id=0, has_side_effects=True, vmem_limit_bytes=VMEM_LIMIT

time: 84.3 us -> 68.8 us (0.82)
  starting transfers between devices: 11.1 us -> 0 us
  local copies, waits for them, and re-layouts: 7.57 us -> 1.36 us
  Pallas kernels: 64.4 us -> 66.5 us
    ppermute x4 -> x0, starting transfers between devices: 11.1 us -> none  [the longest x1 5.51 us: body(): ylo = lax.ppermute(u[:, yc - 1:yc], 'row', up(nr))]
    pallas_call x1, Pallas kernels: 3.4 us -> 11.3 us  [body(): pl.pallas_call(functools.partial(table_kernel, nr, nc), in_specs=[vmem, p...]
    pallas_call x1, Pallas kernels: 26.7 us -> 20.5 us  [body(): pl.pallas_call(functools.partial(exchange_kernel, nr, nc, chunks), in_spe...]
    unnamed x2 -> x0, local copies, waits for them, and re-layouts: 3.38 us -> none
    slice x2 -> x0, local copies, waits for them, and re-layouts: 2.83 us -> none  [the longest x1 1.76 us: body(): yhi = lax.ppermute(u[:, 0:1], 'row', down(nr))]
  transfers between devices with their start and end apart: 4 -> 0, of which waited for: 0 -> 0; matrix products, arithmetic and copies ran while one was open for 5% -> 0% of each run, Pallas kernels for 4% -> 0%
where the time goes in v3:
time: 68.8 us; the launch traced here: 68.6 us
  Pallas kernels  66.5 us (97%)
  local copies, waits for them, and re-layouts  1.36 us (2%)
  other arithmetic  0.7 us (1%)
    pallas_call x1, Pallas kernels, body(): pl.pallas_call(functools.partial(sweep_kernel, planes), grid=(steps,), in...  25.4 us
    pallas_call x1, Pallas kernels, body(): pl.pallas_call(functools.partial(exchange_kernel, nr, nc, chunks), in_spe...  20.5 us
    pallas_call x1, Pallas kernels, body(): pl.pallas_call(functools.partial(table_kernel, nr, nc), in_specs=[vmem, p...  11.3 us
    pallas_call x1, Pallas kernels, body(): pl.pallas_call(functools.partial(finish_kernel, planes), grid=(steps,), i...  9.26 us

profile of v3, /device:TPU:0, one launch (start us, length us, event | category | flops | bytes accessed | tf_op | source)
XLA Modules:
  0.0 68.6 jit_solution(17037354810814783990)
XLA Ops:
  0.0 0.7 pad.11
  0.7 0.7 pad.12
  1.4 0.7 %select_maximum_fusion.faces_ref = f32[8,1024]{1,0:T(8,128)S(1)} fusion(f32[1,1024]{1,0:T(1,128)S(1)} %bitcast.4, f32[1,1024]{1,0:T(1,128)S(1)} %bitcast.3, f32[1,1024]{1,0:T(1,128)} %bitcast.5), kind=kLoop, calls=%fused_computation | loop fusion | flops 49152 | bytes 45056 | tf_op jit(solution)/shard_map/stack | solution.py:475
  2.1 11.3 %shard_map.55 = (bf16[4,256,256]{2,1,0:T(8,128)(2,1)S(1)}, bf16[4,256,256]{2,1,0:T(8,128)(2,1)S(1)}, f32[4,1024]{1,0:T(4,128)S(1)}, f32[64,192]{1,0:T(8,128)S(1)...) custom-call(f32[8,1024]{1,0:T(8,128)S(1)} %select_maximum_fusion.fac, ...), custom_call_target="tpu_custom_call" | custom-call | flops 40000000 | bytes 1048576 | tf_op jit(solution)/shard_map/pallas_call | solution.py:482
  13.4 25.4 %shard_map.56 = (f32[32,64,1024]{2,1,0:T(8,128)S(1)}, f32[2,32,1024]{2,1,0:T(8,128)S(1)}, f32[2,64,1024]{2,1,0:T(8,128)S(1)}) custom-call(f32[16,128]{1,0:T(8,128)S(1)} %get-tuple-element.19.zt_ref, f32[32,64,1024]{2,1,0:T(8,128)S(1)} %get-tuple-element.20.u_ref, f32[2,32,1024]{2,1,0:T(8,128)S(1)} %get-tuple-element.21.yhalo_ref, ...), custom_call_target="tpu_custom_call" | custom-call | tf_op jit(solution)/shard_map/pallas_call | solution.py:519
  38.8 20.5 %shard_map.57 = (f32[2,32,1024]{2,1,0:T(8,128)S(1)}, f32[2,64,1024]{2,1,0:T(8,128)S(1)}) custom-call(f32[16,128]{1,0:T(8,128)S(1)} %get-tuple-element.19.zt_ref, f32[64,128]{1,0:T(8,128)S(1)} %get-tuple-element.23.yt_ref.yp_ref, f32[2,32,1024]{2,1,0:T(8,128)S(1)} %get-tuple-element.29.ye_ref, f32[2,64,1024]{2,1,0:T(8,128)S(1)} %get-tuple-element.30.ze_ref), custom_call_target="tpu_custom_call" | custom-call | tf_op jit(solution)/shard_map/pallas_call | solution.py:536
  59.3 9.3 %shard_map.58 = f32[32,64,1024]{2,1,0:T(8,128)} custom-call(f32[16,128]{1,0:T(8,128)S(1)} %get-tuple-element.19.zt_ref, f32[32,64,1024]{2,1,0:T(8,128)S(1)} %get-tuple-element.20.u_ref, f32[32,64,1024]{2,1,0:T(8,128)S(1)} %get-tuple-element.28.v_ref, f32[64,128]{1,0:T(8,128)S(1)} %get-tuple-element.23.yt_ref.yp_ref, ...), custom_call_target="tpu_custom_call" | custom-call | tf_op jit(solution)/shard_map/pallas_call | solution.py:562

commit v4 on v3

--- a/solution.py
+++ b/solution.py
@@ -56,7 +56,7 @@
 
 
 def table_kernel(
-    nr, nc, faces_ref, field_ref, xh_ref, xl_ref, xp_ref, ym_ref, yt_ref, zt_ref,
+    nr, nc, xf_ref, yf_ref, zf_ref, field_ref, xh_ref, xl_ref, xp_ref, ym_ref, yt_ref, zt_ref,
     held_ref, yhalo_ref, zhalo_ref, strips, edges, fetch_sem, strip_sem, send_sem, recv_sem,
 ):
     row, col = lax.axis_index("row"), lax.axis_index("col")
@@ -122,8 +122,13 @@
             target = ends[k][1]
             target[...] = jnp.zeros_like(target)
 
-    faces = faces_ref[...]
-    length = faces.shape[1]
+    given = [xf_ref[...], yf_ref[...], zf_ref[...]]
+    length = -(-max(a.shape[1] for a in given) // 128) * 128
+    lines = []
+    for a in given:
+        missing = length - a.shape[1]
+        lines.append(jnp.concatenate([a, jnp.zeros((1, missing), a.dtype)], 1) if missing else a)
+    faces = jnp.concatenate(lines + [jnp.zeros((5, length), jnp.float32)], axis=0)
     nb, bx = xh_ref.shape[0], xh_ref.shape[1]
     nx = nb * bx
     here = WEIGHT * STEP * faces
@@ -137,10 +142,12 @@
     ups = running_sum(jnp.log(jnp.maximum(here / (here + h), 1e-30)))
     downs = running_sum(jnp.log(jnp.maximum(down, 1e-30)))
     ups_before, downs_before = shifted(ups, 1, 0.0), shifted(downs, 1, 0.0)
-    next_faces = shifted(faces, -1, 0.0)
-
-    xp_ref[2:3] = faces[0:1, :nx]
-    xp_ref[3:4] = next_faces[0:1, :nx]
+    full, next_full = STEP * faces, STEP * shifted(faces, -1, 0.0)
+    around = full + next_full
+
+    xp_ref[2:3] = shifted(next_full, 1, 0.0)[0:1, :nx]
+    xp_ref[3:4] = next_full[0:1, :nx]
+    xp_ref[4:5] = around[0:1, :nx]
     for b in range(nb):
         first, last = b * bx, (b + 1) * bx - 1
         cols = slice(first, last + 1)
@@ -167,8 +174,8 @@
     ym_ref[:, 0:yc] = high
     ym_ref[:, yc:2 * yc] = high
     ym_ref[:, 2 * yc:3 * yc] = block - high
-    lines = [onward, backward, own(faces, 1, y0), own(next_faces, 1, y0)]
-    lines = [a[:, :wide] for a in lines] + [jnp.zeros((124, wide), jnp.float32)]
+    lines = [onward, backward, own(full, 1, y0), own(next_full, 1, y0), own(around, 1, y0)]
+    lines = [a[:, :wide] for a in lines] + [jnp.zeros((123, wide), jnp.float32)]
     yt_ref[...] = jnp.transpose(jnp.concatenate(lines, axis=0))[:yc]
 
     lane = lax.broadcasted_iota(jnp.int32, (1, 128), 1)
@@ -186,13 +193,14 @@
     over = jnp.where(at == zc - 1, own(diag, 2, z0), own(inverse, 2, z0))
     into = jnp.where(at == 0, 0.0, own(here, 2, z0) * over)
     lines = [
-        over, into, own(down, 2, z0), own(faces, 2, z0), own(next_faces, 2, z0), onward, backward,
+        over, into, own(down, 2, z0), own(full, 2, z0), own(next_full, 2, z0), onward, backward,
     ]
     for k, line in enumerate(lines):
         zt_ref[k:k + 1] = line[:, :128]
     zt_ref[7:8] = low_weights
     zt_ref[8:9] = high_weights
-    zt_ref[9:16] = jnp.zeros((7, 128), jnp.float32)
+    zt_ref[9:10] = own(around, 2, z0)[:, :128]
+    zt_ref[10:16] = jnp.zeros((6, 128), jnp.float32)
     for k in range(4):
         @pl.when(places[k][0])
         def _():
@@ -227,7 +235,6 @@
     nb, bx = xh_ref.shape[0], xh_ref.shape[1]
     kx, kxn = xp_ref[2:3], xp_ref[3:4]
     ky, kyn = yt_ref[:, 2:3], yt_ref[:, 3:4]
-    lane = lax.broadcasted_iota(jnp.int32, (yc, nx), 1)
     sub = lax.broadcasted_iota(jnp.int32, (yc, nx), 0)
 
     @pl.when(step == 0)
@@ -242,15 +249,13 @@
         z = step * planes + p
         u = u_ref[z]
         above = u_ref[z + 1] if p + 1 < planes else above_last
-        left = jnp.where(lane == 0, 0.0, pltpu.roll(u, 1, 1))
-        right = pltpu.roll(u, nx - 1, 1)
         down = jnp.where(sub == 0, yhalo_ref[0, pl.ds(z, 1)], pltpu.roll(u, 1, 0))
         upper = jnp.where(sub == yc - 1, yhalo_ref[1, pl.ds(z, 1)], pltpu.roll(u, yc - 1, 0))
-        total = kxn * (right - u) - kx * (u - left)
-        total += kyn * (upper - u) - ky * (u - down)
-        total += zt_ref[4, z] * (above - u) - zt_ref[3, z] * (u - below)
-        total += rea_ref[p] * u * (1.0 - u * u)
-        changes.append(STEP * total)
+        total = kxn * pltpu.roll(u, nx - 1, 1) + kx * pltpu.roll(u, 1, 1)
+        total += kyn * upper + ky * down
+        total += zt_ref[4, z] * above + zt_ref[3, z] * below
+        centre = STEP * rea_ref[p] * (1.0 - u * u) - (xp_ref[4:5] + (yt_ref[:, 4:5] + zt_ref[9, z]))
+        changes.append(total + u * centre)
         below = u
     change = jnp.concatenate(changes, axis=0) if planes > 1 else changes[0]
     local = []
@@ -468,12 +473,8 @@
 def body(u, reaction, x_faces, y_faces, z_faces, x_inverse, y_inverse, z_inverse):
     zc, yc, nx = u.shape
     nr, nc = lax.axis_size("row"), lax.axis_size("col")
-    ny, nz = y_faces.shape[0], z_faces.shape[0]
     f32 = jnp.float32
 
-    longest = -(-max(nx, ny, nz) // 128) * 128
-    faces = jnp.stack([jnp.pad(f, (0, longest - f.shape[0])) for f in (x_faces, y_faces, z_faces)])
-    faces = jnp.pad(faces, ((0, 5), (0, 0)))
     tall = 8 if yc % 8 == 0 else yc
     bx = 256 if nx % 256 == 0 else nx
     nb = nx // bx
@@ -481,12 +482,12 @@
     vmem = pl.BlockSpec(memory_space=pltpu.VMEM)
     xh, xl, xp, ym, yt, zt, held, yhalo, zhalo = pl.pallas_call(
         functools.partial(table_kernel, nr, nc),
-        in_specs=[vmem, pl.BlockSpec(memory_space=pltpu.HBM)],
+        in_specs=[vmem, vmem, vmem, pl.BlockSpec(memory_space=pltpu.HBM)],
         out_specs=[vmem] * 9,
         out_shape=[
             jax.ShapeDtypeStruct((nb, bx, bx), jnp.bfloat16),
             jax.ShapeDtypeStruct((nb, bx, bx), jnp.bfloat16),
-            jax.ShapeDtypeStruct((4, nx), f32),
+            jax.ShapeDtypeStruct((8, nx), f32),
             jax.ShapeDtypeStruct((yc, 3 * yc), f32),
             jax.ShapeDtypeStruct((yc, 128), f32),
             jax.ShapeDtypeStruct((16, 128), f32),
@@ -506,24 +507,21 @@
             collective_id=1, has_side_effects=True, vmem_limit_bytes=VMEM_LIMIT
         ),
         cost_estimate=pl.CostEstimate(flops=40000000, bytes_accessed=1 << 20, transcendentals=0),
-    )(faces, pltpu.with_memory_space_constraint(u, pltpu.HBM))
-
-    planes = 2 if zc % 2 == 0 else 1
-    steps = zc // planes
+    )(x_faces[None], y_faces[None], z_faces[None], pltpu.with_memory_space_constraint(u, pltpu.HBM))
+
+    planes = next(p for p in (4, 2, 1) if zc % p == 0)
+    last = next(p for p in (8, 4, 2, 1) if zc % p == 0)
     reaction = pltpu.with_memory_space_constraint(reaction, pltpu.HBM)
 
-    def whole(*shape):
-        return pl.BlockSpec(shape, lambda s: (0,) * len(shape))
-
-    slab = pl.BlockSpec((planes, yc, nx), lambda s: (s, 0, 0))
+    slab = pl.BlockSpec((planes, yc, nx), lambda step: (step, 0, 0))
     v, ye, ze = pl.pallas_call(
         functools.partial(sweep_kernel, planes),
-        grid=(steps,),
+        grid=(zc // planes,),
         in_specs=[
             smem, vmem, vmem, vmem, slab,
-            whole(yc, 128), whole(nb, bx, bx), whole(nb, bx, bx), whole(4, nx), whole(yc, 3 * yc),
-        ],
-        out_specs=[vmem, whole(2, zc, nx), whole(2, yc, nx)],
+            vmem, vmem, vmem, vmem, vmem,
+        ],
+        out_specs=[vmem, vmem, vmem],
         out_shape=[
             on_chip(zc, yc, nx),
             jax.ShapeDtypeStruct((2, zc, nx), f32),
@@ -560,10 +558,10 @@
     )(zt, yt, ye, ze)
 
     return pl.pallas_call(
-        functools.partial(finish_kernel, planes),
-        grid=(steps,),
-        in_specs=[smem, vmem, vmem, whole(yc, 128), whole(2, zc, nx), whole(2, yc, nx)],
-        out_specs=slab,
+        functools.partial(finish_kernel, last),
+        grid=(zc // last,),
+        in_specs=[smem, vmem, vmem, vmem, vmem, vmem],
+        out_specs=pl.BlockSpec((last, yc, nx), lambda step: (step, 0, 0)),
         out_shape=jax.ShapeDtypeStruct((zc, yc, nx), f32),
         compiler_params=pltpu.CompilerParams(vmem_limit_bytes=VMEM_LIMIT),
     )(zt, held, v, yt, sy, sz)

time: 68.8 us -> 62.9 us (0.914)
  Pallas kernels: 66.5 us -> 60.6 us
  other arithmetic: 0.7 us -> 0 us
    pallas_call x3, Pallas kernels: 45.9 us -> 40 us  [the longest x1 21.6 us: body(): pl.pallas_call(functools.partial(sweep_kernel, planes), grid=(zc // plane...]
    unnamed x0 -> x6, local copies, waits for them, and re-layouts: none -> 2.04 us
    pad x2 -> x0, local copies, waits for them, and re-layouts: 1.36 us -> none  [body(): jnp.pad(f, (0, longest - f.shape[0]))]
    another operation x1 -> x0, other arithmetic: 0.7 us -> none  [body(): jnp.stack([jnp.pad(f, (0, longest - f.shape[0])) for f in (x_faces, y_fac...]
where the time goes in v4:
time: 62.9 us; the launch traced here: 62.7 us
  Pallas kernels  60.6 us (96%)
  local copies, waits for them, and re-layouts  2.04 us (3%)
    pallas_call x1, Pallas kernels, body(): pl.pallas_call(functools.partial(sweep_kernel, planes), grid=(zc // plane...  21.6 us
    pallas_call x1, Pallas kernels, body(): pl.pallas_call(functools.partial(exchange_kernel, nr, nc, chunks), in_spe...  20.6 us
    pallas_call x1, Pallas kernels, body(): pl.pallas_call(functools.partial(table_kernel, nr, nc), in_specs=[vmem, v...  11.3 us
    pallas_call x1, Pallas kernels, body(): pl.pallas_call(functools.partial(finish_kernel, last), grid=(zc // last,)...  7.12 us
    unnamed x6, local copies, waits for them, and re-layouts  2.04 us

profile of v4, /device:TPU:0, one launch (start us, length us, event | category | flops | bytes accessed | tf_op | source)
XLA Modules:
  0.0 62.7 jit_solution(6521355644432227434)
XLA Ops:
  0.0 0.0 copy-start
  0.0 0.7 %copy-done = f32[1024]{0:T(1024)S(1)} copy-done((f32[1024]{0:T(1024)S(1)}, f32[1024]{0:T(1024)}, u32[]{:S(2)}) %copy-start) | copy-done | bytes 4120
  0.7 0.0 copy-start.1
  0.7 0.7 %copy-done.1 = f32[256]{0:T(256)S(1)} copy-done((f32[256]{0:T(256)S(1)}, f32[256]{0:T(256)}, u32[]{:S(2)}) %copy-start.1) | copy-done | bytes 1048
  1.4 0.0 copy-start.2
  1.4 0.7 %copy-done.2 = f32[256]{0:T(256)S(1)} copy-done((f32[256]{0:T(256)S(1)}, f32[256]{0:T(256)}, u32[]{:S(2)}) %copy-start.2) | copy-done | bytes 1048
  2.0 11.3 %shard_map.55 = (bf16[4,256,256]{2,1,0:T(8,128)(2,1)S(1)}, bf16[4,256,256]{2,1,0:T(8,128)(2,1)S(1)}, f32[8,1024]{1,0:T(8,128)S(1)}, f32[64,192]{1,0:T(8,128)S(1)...) custom-call(f32[1,1024]{1,0:T(1,128)S(1)} %bitcast.3, ...), custom_call_target="tpu_custom_call" | custom-call | flops 40000000 | bytes 1048576 | tf_op jit(solution)/shard_map/pallas_call | solution.py:483
  13.3 21.6 %shard_map.56 = (f32[32,64,1024]{2,1,0:T(8,128)S(1)}, f32[2,32,1024]{2,1,0:T(8,128)S(1)}, f32[2,64,1024]{2,1,0:T(8,128)S(1)}) custom-call(f32[16,128]{1,0:T(8,128)S(1)} %get-tuple-element.19.zt_ref, f32[32,64,1024]{2,1,0:T(8,128)S(1)} %get-tuple-element.20.u_ref, f32[2,32,1024]{2,1,0:T(8,128)S(1)} %get-tuple-element.21.yhalo_ref, ...), custom_call_target="tpu_custom_call" | custom-call | tf_op jit(solution)/shard_map/pallas_call | solution.py:517
  35.0 20.6 %shard_map.57 = (f32[2,32,1024]{2,1,0:T(8,128)S(1)}, f32[2,64,1024]{2,1,0:T(8,128)S(1)}) custom-call(f32[16,128]{1,0:T(8,128)S(1)} %get-tuple-element.19.zt_ref, f32[64,128]{1,0:T(8,128)S(1)} %get-tuple-element.23.yt_ref.yp_ref, f32[2,32,1024]{2,1,0:T(8,128)S(1)} %get-tuple-element.29.ye_ref, f32[2,64,1024]{2,1,0:T(8,128)S(1)} %get-tuple-element.30.ze_ref), custom_call_target="tpu_custom_call" | custom-call | tf_op jit(solution)/shard_map/pallas_call | solution.py:534
  55.5 7.1 %shard_map.58 = f32[32,64,1024]{2,1,0:T(8,128)} custom-call(f32[16,128]{1,0:T(8,128)S(1)} %get-tuple-element.19.zt_ref, f32[32,64,1024]{2,1,0:T(8,128)S(1)} %get-tuple-element.20.u_ref, f32[32,64,1024]{2,1,0:T(8,128)S(1)} %get-tuple-element.28.v_ref, f32[64,128]{1,0:T(8,128)S(1)} %get-tuple-element.23.yt_ref.yp_ref, ...), custom_call_target="tpu_custom_call" | custom-call | tf_op jit(solution)/shard_map/pallas_call | solution.py:560
Async XLA Ops:
  0.0 0.7 %copy-start = (f32[1024]{0:T(1024)S(1)}, f32[1024]{0:T(1024)}, u32[]{:S(2)}) copy-start(f32[1024]{0:T(1024)} %param.10) | copy-start | bytes 12292
  0.7 0.7 %copy-start.1 = (f32[256]{0:T(256)S(1)}, f32[256]{0:T(256)}, u32[]{:S(2)}) copy-start(f32[256]{0:T(256)} %param.11) | copy-start | bytes 3076
  1.4 0.7 %copy-start.2 = (f32[256]{0:T(256)S(1)}, f32[256]{0:T(256)}, u32[]{:S(2)}) copy-start(f32[256]{0:T(256)} %param.12) | copy-start | bytes 3076

commit v5 on v4

--- a/solution.py
+++ b/solution.py
@@ -509,7 +509,7 @@
         cost_estimate=pl.CostEstimate(flops=40000000, bytes_accessed=1 << 20, transcendentals=0),
     )(x_faces[None], y_faces[None], z_faces[None], pltpu.with_memory_space_constraint(u, pltpu.HBM))
 
-    planes = next(p for p in (4, 2, 1) if zc % p == 0)
+    planes = next(p for p in (8, 4, 2, 1) if zc % p == 0)
     last = next(p for p in (8, 4, 2, 1) if zc % p == 0)
     reaction = pltpu.with_memory_space_constraint(reaction, pltpu.HBM)
 

time: 62.9 us -> 61.8 us (0.983)
  Pallas kernels: 60.6 us -> 59.5 us
    pallas_call x1, Pallas kernels: 21.6 us -> 20.5 us  [body(): pl.pallas_call(functools.partial(sweep_kernel, planes), grid=(zc // plane...]
where the time goes in v5:
time: 61.8 us; the launch traced here: 61.5 us
  Pallas kernels  59.5 us (96%)
  local copies, waits for them, and re-layouts  2.04 us (3%)
    pallas_call x1, Pallas kernels, body(): pl.pallas_call(functools.partial(exchange_kernel, nr, nc, chunks), in_spe...  20.6 us
    pallas_call x1, Pallas kernels, body(): pl.pallas_call(functools.partial(sweep_kernel, planes), grid=(zc // plane...  20.5 us
    pallas_call x1, Pallas kernels, body(): pl.pallas_call(functools.partial(table_kernel, nr, nc), in_specs=[vmem, v...  11.3 us
    pallas_call x1, Pallas kernels, body(): pl.pallas_call(functools.partial(finish_kernel, last), grid=(zc // last,)...  7.12 us
    unnamed x6, local copies, waits for them, and re-layouts  2.04 us

profile of v5, /device:TPU:0, one launch (start us, length us, event | category | flops | bytes accessed | tf_op | source)
XLA Modules:
  0.0 61.5 jit_solution(11054574599516732450)
XLA Ops:
  0.0 0.0 copy-start
  0.0 0.7 %copy-done = f32[1024]{0:T(1024)S(1)} copy-done((f32[1024]{0:T(1024)S(1)}, f32[1024]{0:T(1024)}, u32[]{:S(2)}) %copy-start) | copy-done | bytes 4120
  0.7 0.0 copy-start.1
  0.7 0.7 %copy-done.1 = f32[256]{0:T(256)S(1)} copy-done((f32[256]{0:T(256)S(1)}, f32[256]{0:T(256)}, u32[]{:S(2)}) %copy-start.1) | copy-done | bytes 1048
  1.4 0.0 copy-start.2
  1.4 0.7 %copy-done.2 = f32[256]{0:T(256)S(1)} copy-done((f32[256]{0:T(256)S(1)}, f32[256]{0:T(256)}, u32[]{:S(2)}) %copy-start.2) | copy-done | bytes 1048
  2.0 11.3 %shard_map.55 = (bf16[4,256,256]{2,1,0:T(8,128)(2,1)S(1)}, bf16[4,256,256]{2,1,0:T(8,128)(2,1)S(1)}, f32[8,1024]{1,0:T(8,128)S(1)}, f32[64,192]{1,0:T(8,128)S(1)...) custom-call(f32[1,1024]{1,0:T(1,128)S(1)} %bitcast.3, ...), custom_call_target="tpu_custom_call" | custom-call | flops 40000000 | bytes 1048576 | tf_op jit(solution)/shard_map/pallas_call | solution.py:483
  13.3 20.5 %shard_map.56 = (f32[32,64,1024]{2,1,0:T(8,128)S(1)}, f32[2,32,1024]{2,1,0:T(8,128)S(1)}, f32[2,64,1024]{2,1,0:T(8,128)S(1)}) custom-call(f32[16,128]{1,0:T(8,128)S(1)} %get-tuple-element.19.zt_ref, f32[32,64,1024]{2,1,0:T(8,128)S(1)} %get-tuple-element.20.u_ref, f32[2,32,1024]{2,1,0:T(8,128)S(1)} %get-tuple-element.21.yhalo_ref, ...), custom_call_target="tpu_custom_call" | custom-call | tf_op jit(solution)/shard_map/pallas_call | solution.py:517
  33.8 20.6 %shard_map.57 = (f32[2,32,1024]{2,1,0:T(8,128)S(1)}, f32[2,64,1024]{2,1,0:T(8,128)S(1)}) custom-call(f32[16,128]{1,0:T(8,128)S(1)} %get-tuple-element.19.zt_ref, f32[64,128]{1,0:T(8,128)S(1)} %get-tuple-element.23.yt_ref.yp_ref, f32[2,32,1024]{2,1,0:T(8,128)S(1)} %get-tuple-element.29.ye_ref, f32[2,64,1024]{2,1,0:T(8,128)S(1)} %get-tuple-element.30.ze_ref), custom_call_target="tpu_custom_call" | custom-call | tf_op jit(solution)/shard_map/pallas_call | solution.py:534
  54.4 7.1 %shard_map.58 = f32[32,64,1024]{2,1,0:T(8,128)} custom-call(f32[16,128]{1,0:T(8,128)S(1)} %get-tuple-element.19.zt_ref, f32[32,64,1024]{2,1,0:T(8,128)S(1)} %get-tuple-element.20.u_ref, f32[32,64,1024]{2,1,0:T(8,128)S(1)} %get-tuple-element.28.v_ref, f32[64,128]{1,0:T(8,128)S(1)} %get-tuple-element.23.yt_ref.yp_ref, ...), custom_call_target="tpu_custom_call" | custom-call | tf_op jit(solution)/shard_map/pallas_call | solution.py:560
Async XLA Ops:
  0.0 0.7 %copy-start = (f32[1024]{0:T(1024)S(1)}, f32[1024]{0:T(1024)}, u32[]{:S(2)}) copy-start(f32[1024]{0:T(1024)} %param.10) | copy-start | bytes 12292
  0.7 0.7 %copy-start.1 = (f32[256]{0:T(256)S(1)}, f32[256]{0:T(256)}, u32[]{:S(2)}) copy-start(f32[256]{0:T(256)} %param.11) | copy-start | bytes 3076
  1.4 0.7 %copy-start.2 = (f32[256]{0:T(256)S(1)}, f32[256]{0:T(256)}, u32[]{:S(2)}) copy-start(f32[256]{0:T(256)} %param.12) | copy-start | bytes 3076
